TPU v7x, 32 devices: a whole 2x2x4 slice. The times are simulated.
32 devices in a mesh: groups: 2 (over x), seq: 16 (over z, y, core).
Axes of the slice: x: 2, y: 2, z: 4, core: 2. Of those that a mesh axis runs over, the one named last changes fastest.
Arguments:
- queries: bfloat16 [64, 4, 8192], P(('groups', 'seq')), parts along dimension 0, may hold values from -128 to 128
- step_keys: bfloat16 [64, 4, 1024], P(('groups', 'seq')), parts along dimension 0, may hold values from -15 to 15
- step_values: bfloat16 [64, 4, 1024], P(('groups', 'seq')), parts along dimension 0, may hold values from -48 to 48
- sample_keys: bfloat16 [64, 1024, 1024], P(('groups', 'seq')), parts along dimension 0, may hold values from -6 to 6
- sample_values: bfloat16 [64, 1024, 1024], P(('groups', 'seq')), parts along dimension 0, may hold values from -48 to 48
- suffix_len: int32 [64], P(('groups', 'seq')), parts along dimension 0, may hold values from 128 to 1024
- prompt_id: int32 [64], P(('groups', 'seq')), parts along dimension 0, may hold values from 0 to 1, as said below
- document_keys: bfloat16 [4, 4096, 1024], P('groups', 'seq'), parts along dimension 0, may hold values from -6 to 6
- document_values: bfloat16 [4, 4096, 1024], P('groups', 'seq'), parts along dimension 0, may hold values from -48 to 48
Outputs:
- attended: bfloat16 [64, 4, 8192], P(('groups', 'seq')), parts along dimension 0
There are 2 independent parts, one for each index of `groups`. A program takes and returns all parts, laid end to end along the dimension named above; each array names one. Nothing has to cross between parts.
Inputs may be any that keep to these rules, and one draw needn't show every extreme that they name: `prompt_id`: each prompt id is held by exactly 16 samples.
All inputs are finite; a program needn't handle non-finite values.
Results may differ from a plain program's by a relative error of at most 0.0013.
Values may be sent and summed in bfloat16 or wider, within the bound.
No kernel may reach another device: no remote copies, remote signals or barrier semaphores. Data moves between devices by JAX's collectives and lax.ppermute only.
A program may use at most 192 MiB of HBM per device.

v0:
```python
import functools
import math

import jax
import jax.numpy as jnp
from jax import lax
from jax.experimental import pallas as pl
from jax.experimental.pallas import tpu as pltpu
from jax.sharding import PartitionSpec as P


QUERY_HEADS = 64
KEY_VALUE_HEADS = 8
HEAD_SIZE = 128
GROUP = QUERY_HEADS // KEY_VALUE_HEADS
SCALING = HEAD_SIZE ** (-0.5)
LANES = 128
EARLY = (6, 7)
LATE = (4, 2, 5, 3, 1)
LIMIT = pltpu.CompilerParams(vmem_limit_bytes=24 * 1024 * 1024)
WEIGHT_SCALE = SCALING * math.log2(math.e)


def whole(space=pltpu.VMEM):
    return pl.BlockSpec(memory_space=space)


def near(array):
    return pltpu.with_memory_space_constraint(array, pltpu.VMEM)


def far(array):
    return pltpu.with_memory_space_constraint(array, pltpu.HBM)


def slice_kernel(partners, keys_ref, values_ref, *refs):
    out_refs, sem = refs[:-1], refs[-1]
    mine = lax.axis_index("seq") % KEY_VALUE_HEADS
    copies = []
    for slot, partner in enumerate(partners):
        head = jnp.bitwise_xor(mine, partner)
        columns = pl.ds(pl.multiple_of(head * HEAD_SIZE, HEAD_SIZE), HEAD_SIZE)
        for side, source in enumerate((keys_ref, values_ref)):
            copy = pltpu.make_async_copy(
                source.at[:, :, columns], out_refs[slot].at[side], sem.at[slot, side]
            )
            copy.start()
            copies.append(copy)
    for copy in copies:
        copy.wait()


def head_slices(keys, values, partners):
    prompts, block, _ = keys.shape
    piece = jax.ShapeDtypeStruct((2, prompts, block, HEAD_SIZE), keys.dtype)
    pieces = pl.pallas_call(
        functools.partial(slice_kernel, partners),
        out_shape=[piece] * len(partners),
        in_specs=[whole(pltpu.HBM)] * 2,
        out_specs=[whole()] * len(partners),
        scratch_shapes=[pltpu.SemaphoreType.DMA((len(partners), 2))],
        compiler_params=LIMIT,
        name="head_slices",
    )(far(keys), far(values))
    return pieces


def pack_kernel(ids_ref, queries_ref, out_ref):
    owned, steps, _ = queries_ref.shape
    rows = owned * steps * GROUP
    lane = lax.broadcasted_iota(jnp.int32, (out_ref.shape[1] - rows, LANES), 1)
    marks = jnp.zeros(lane.shape, jnp.float32)
    for n in range(owned):
        marks = jnp.where(lane == n, ids_ref[n].astype(jnp.float32), marks)
    marks = marks.astype(jnp.bfloat16)
    for head in range(KEY_VALUE_HEADS):
        parts = []
        for n in range(owned):
            for r in range(GROUP):
                first = (head * GROUP + r) * HEAD_SIZE
                parts.append(queries_ref[n, :, first : first + HEAD_SIZE].astype(jnp.float32))
        block = jnp.concatenate(parts, axis=0).astype(jnp.bfloat16)
        for copy in range(out_ref.shape[0] // KEY_VALUE_HEADS):
            out_ref[copy * KEY_VALUE_HEADS + head, :rows, :] = block
            out_ref[copy * KEY_VALUE_HEADS + head, rows:, :] = marks


def pack_queries(queries, prompt_id, device_count):
    owned, steps, _ = queries.shape
    rows = owned * steps * GROUP
    packed = pl.pallas_call(
        pack_kernel,
        out_shape=jax.ShapeDtypeStruct((device_count, rows + 16, HEAD_SIZE), jnp.bfloat16),
        in_specs=[whole(pltpu.SMEM), whole()],
        out_specs=whole(),
        compiler_params=LIMIT,
        name="pack_queries",
    )(far(prompt_id), far(queries))
    return packed


def contract(left, right, dims):
    return lax.dot_general(left, right, (dims, ((), ())), preferred_element_type=jnp.float32)


def diagonal(rows):
    row = lax.broadcasted_iota(jnp.int32, (rows, LANES), 0)
    lane = lax.broadcasted_iota(jnp.int32, (rows, LANES), 1)
    return (lane == row) | (lane == row + rows)


def diagonal_row(columns, mask):
    return jnp.sum(jnp.where(mask, columns, 0.0), axis=0, keepdims=True)


def max_and_total(peak, total):
    rows = peak.shape[0]
    lane = lax.broadcasted_iota(jnp.int32, (rows, LANES), 1)
    return jnp.where(lane < LANES // 2, peak, total)


def suffix_kernel(len_ref, query_ref, keys_ref, values_ref, new_keys_ref, new_values_ref, out_ref, aux_ref):
    owned, _, _ = keys_ref.shape
    steps = new_keys_ref.shape[1]
    rows = steps * GROUP
    aux_parts = []
    for n in range(owned):
        query = query_ref[0, n * rows : (n + 1) * rows, :]
        cache = contract(query, keys_ref[n], ((1,), (1,))) * SCALING
        fresh = contract(query, new_keys_ref[n], ((1,), (1,))) * SCALING
        cache_live = lax.broadcasted_iota(jnp.int32, cache.shape, 1) < len_ref[n]
        fresh_live = (
            lax.broadcasted_iota(jnp.int32, fresh.shape, 1)
            <= lax.broadcasted_iota(jnp.int32, fresh.shape, 0) % steps
        )
        peak = jnp.maximum(
            jnp.max(jnp.where(cache_live, cache, -jnp.inf), axis=1, keepdims=True),
            jnp.max(jnp.where(fresh_live, fresh, -jnp.inf), axis=1, keepdims=True),
        )
        cache_exp = jnp.where(cache_live, jnp.exp(cache - peak), 0.0)
        fresh_exp = jnp.where(fresh_live, jnp.exp(fresh - peak), 0.0)
        total = jnp.sum(cache_exp, axis=1, keepdims=True) + jnp.sum(fresh_exp, axis=1, keepdims=True)
        out = contract(cache_exp.astype(jnp.bfloat16), values_ref[n], ((1,), (0,))) + contract(
            fresh_exp.astype(jnp.bfloat16), new_values_ref[n], ((1,), (0,))
        )
        out_ref[0, n * rows : (n + 1) * rows, :] = out
        aux_parts.append(max_and_total(peak, total))
    aux_ref[0] = diagonal_row(jnp.concatenate(aux_parts, axis=0), diagonal(owned * rows))


def suffix_part(suffix_len, packed, keys, values, new_keys, new_values):
    owned, slots, _ = keys.shape
    steps = new_keys.shape[1]
    rows = owned * steps * GROUP
    return pl.pallas_call(
        suffix_kernel,
        grid_spec=pltpu.PrefetchScalarGridSpec(
            num_scalar_prefetch=1,
            grid=(KEY_VALUE_HEADS,),
            in_specs=[
                pl.BlockSpec((1, packed.shape[1], HEAD_SIZE), lambda h, _: (h, 0, 0)),
                pl.BlockSpec((owned, slots, HEAD_SIZE), lambda h, _: (0, 0, h)),
                pl.BlockSpec((owned, slots, HEAD_SIZE), lambda h, _: (0, 0, h)),
                pl.BlockSpec((owned, steps, HEAD_SIZE), lambda h, _: (0, 0, h)),
                pl.BlockSpec((owned, steps, HEAD_SIZE), lambda h, _: (0, 0, h)),
            ],
            out_specs=[
                pl.BlockSpec((1, rows, HEAD_SIZE), lambda h, _: (h, 0, 0)),
                pl.BlockSpec((1, 1, LANES), lambda h, _: (h, 0, 0)),
            ],
        ),
        out_shape=[
            jax.ShapeDtypeStruct((KEY_VALUE_HEADS, rows, HEAD_SIZE), jnp.float32),
            jax.ShapeDtypeStruct((KEY_VALUE_HEADS, 1, LANES), jnp.float32),
        ],
        compiler_params=LIMIT,
        name="suffix_part",
    )(suffix_len, packed, keys, values, new_keys, new_values)


def attend(query, pieces, prompt, state):
    for piece in pieces:
        score = contract(query, piece[0, prompt], ((1,), (1,)))
        peak = jnp.max(score, axis=1, keepdims=True)
        weight = jnp.exp2((score - peak) * WEIGHT_SCALE)
        total = jnp.sum(weight, axis=1, keepdims=True)
        part = contract(weight.astype(jnp.bfloat16), piece[1, prompt], ((1,), (0,)))
        peak = jnp.broadcast_to(peak * SCALING, part.shape)
        total = jnp.broadcast_to(total, part.shape)
        if state is None:
            state = (peak, total, part)
        else:
            best, mass, acc = state
            top = jnp.maximum(best, peak)
            old = jnp.exp(best - top)
            new = jnp.exp(peak - top)
            state = (top, mass * old + total * new, acc * old + part * new)
    return state


def find_places(ids_ref, place_ref, count_ref, rows):
    samples = ids_ref.shape[0]
    prompts = count_ref.shape[0]
    per_prompt = samples // prompts
    for p in range(prompts):
        count_ref[p] = 0

    def one(sample, carry):
        prompt = ids_ref[sample]
        rank = count_ref[prompt]
        count_ref[prompt] = rank + 1
        place_ref[sample] = (prompt * per_prompt + rank) * rows
        return carry

    lax.fori_loop(0, samples, one, 0, unroll=8)


def first_kernel(rows, chunk, ids_ref, queries_ref, *refs):
    pieces, refs = refs[:-6], refs[-6:]
    sorted_ref, out_ref, peak_ref, total_ref, place_ref, count_ref = refs
    devices = queries_ref.shape[0]
    owned = ids_ref.shape[0] // devices
    prompts = count_ref.shape[0]
    find_places(ids_ref, place_ref, count_ref, rows)

    def sort_one(device, carry):
        for n in range(owned):
            target = pl.ds(pl.multiple_of(place_ref[device * owned + n], rows), rows)
            sorted_ref[target, :] = queries_ref[device, n * rows : (n + 1) * rows, :]
        return carry

    lax.fori_loop(0, devices, sort_one, 0, unroll=4)
    chunks = sorted_ref.shape[0] // prompts // chunk

    def step(index, carry):
        target = pl.ds(pl.multiple_of(index * chunk, chunk), chunk)
        peak, total, out = attend(sorted_ref[target, :], pieces, index // chunks, None)
        out_ref[target, :] = out
        peak_ref[target, :] = peak
        total_ref[target, :] = total
        return carry

    lax.fori_loop(0, prompts * chunks, step, 0)


def next_kernel(chunk, sorted_ref, acc_in, peak_in, total_in, *refs):
    pieces, (acc_ref, peak_ref, total_ref) = refs[:-3], refs[-3:]
    prompts = pieces[0].shape[1]
    chunks = sorted_ref.shape[0] // prompts // chunk

    def step(index, carry):
        target = pl.ds(pl.multiple_of(index * chunk, chunk), chunk)
        state = (peak_in[target, :], total_in[target, :], acc_in[target, :])
        peak, total, out = attend(sorted_ref[target, :], pieces, index // chunks, state)
        acc_ref[target, :] = out
        peak_ref[target, :] = peak
        total_ref[target, :] = total
        return carry

    lax.fori_loop(0, prompts * chunks, step, 0)


def last_kernel(rows, chunk, ids_ref, sorted_ref, acc_ref, peak_ref, total_ref, *refs):
    pieces, refs = refs[:-5], refs[-5:]
    out_ref, out_scratch, aux_scratch, place_ref, count_ref = refs
    devices = out_ref.shape[0]
    owned = ids_ref.shape[0] // devices
    prompts = count_ref.shape[0]
    find_places(ids_ref, place_ref, count_ref, rows)
    chunks = sorted_ref.shape[0] // prompts // chunk

    def step(index, carry):
        target = pl.ds(pl.multiple_of(index * chunk, chunk), chunk)
        state = (peak_ref[target, :], total_ref[target, :], acc_ref[target, :])
        peak, total, out = attend(sorted_ref[target, :], pieces, index // chunks, state)
        out_scratch[target, :] = out
        aux_scratch[target, :] = max_and_total(peak, total)
        return carry

    lax.fori_loop(0, prompts * chunks, step, 0)

    mask = diagonal(owned * rows)

    def emit(device, carry):
        aux_parts = []
        for n in range(owned):
            source = pl.ds(pl.multiple_of(place_ref[device * owned + n], rows), rows)
            out_ref[device, n * rows : (n + 1) * rows, :] = out_scratch[source, :]
            aux_parts.append(aux_scratch[source, :])
        row = diagonal_row(jnp.concatenate(aux_parts, axis=0), mask)
        out_ref[device, owned * rows :, :] = jnp.broadcast_to(row, (8, LANES))
        return carry

    lax.fori_loop(0, devices, emit, 0, unroll=4)


def first_stage(ids, queries, pieces, rows):
    samples = ids.shape[0]
    prompts = pieces[0].shape[1]
    total = samples * rows
    results = pl.pallas_call(
        functools.partial(first_kernel, rows, min(256, total // prompts)),
        out_shape=[
            jax.ShapeDtypeStruct((total, HEAD_SIZE), jnp.bfloat16),
            jax.ShapeDtypeStruct((total, HEAD_SIZE), jnp.float32),
            jax.ShapeDtypeStruct((total, LANES), jnp.float32),
            jax.ShapeDtypeStruct((total, LANES), jnp.float32),
        ],
        in_specs=[whole(pltpu.SMEM)] + [whole()] * (1 + len(pieces)),
        out_specs=[whole()] * 4,
        scratch_shapes=[pltpu.SMEM((samples,), jnp.int32), pltpu.SMEM((prompts,), jnp.int32)],
        compiler_params=LIMIT,
        name="first_stage",
    )(ids, queries, *pieces)
    return [near(result) for result in results]


def next_stage(state, pieces):
    total = state[0].shape[0]
    prompts = pieces[0].shape[1]
    results = pl.pallas_call(
        functools.partial(next_kernel, min(256, total // prompts)),
        out_shape=[jax.ShapeDtypeStruct((total, HEAD_SIZE), jnp.float32)] * 3,
        in_specs=[whole()] * (4 + len(pieces)),
        out_specs=[whole()] * 3,
        compiler_params=LIMIT,
        name="next_stage",
    )(*state, *pieces)
    return [state[0]] + [near(result) for result in results]


def last_stage(ids, state, pieces, rows, devices):
    samples = ids.shape[0]
    prompts = pieces[0].shape[1]
    total = samples * rows
    return (
        pl.pallas_call(
            functools.partial(last_kernel, rows, min(256, total // prompts)),
            out_shape=jax.ShapeDtypeStruct((devices, total // devices + 8, HEAD_SIZE), jnp.float32),
            in_specs=[whole(pltpu.SMEM)] + [whole()] * (4 + len(pieces)),
            out_specs=whole(),
            scratch_shapes=[
                pltpu.VMEM((total, HEAD_SIZE), jnp.float32),
                pltpu.VMEM((total, HEAD_SIZE), jnp.float32),
                pltpu.SMEM((samples,), jnp.int32),
                pltpu.SMEM((prompts,), jnp.int32),
            ],
            compiler_params=LIMIT,
            name="last_stage",
        )(ids, *state, *pieces)
    )


def merge_kernel(got_ref, local_ref, local_aux_ref, out_ref):
    owned, steps, _ = out_ref.shape
    rows = local_ref.shape[1]
    half = LANES // 2
    groups = got_ref.shape[0] // KEY_VALUE_HEADS
    aux = [local_aux_ref[:, 0, :]]
    for g in range(groups):
        aux.append(
            jnp.concatenate(
                [got_ref[g * KEY_VALUE_HEADS + h, rows : rows + 1, :] for h in range(KEY_VALUE_HEADS)],
                axis=0,
            )
        )
    peaks = [a[:, :half] for a in aux]
    totals = [a[:, half:] for a in aux]
    highest = functools.reduce(jnp.maximum, peaks)
    scales = [jnp.exp(peak - highest) for peak in peaks]
    denominator = functools.reduce(jnp.add, [t * s for t, s in zip(totals, scales)])
    factors = [jnp.transpose(s / denominator) for s in scales]
    for h in range(KEY_VALUE_HEADS):
        result = local_ref[h] * factors[0][:, h : h + 1]
        for g in range(groups):
            result += got_ref[g * KEY_VALUE_HEADS + h, :rows, :] * factors[g + 1][:, h : h + 1]
        for n in range(owned):
            for r in range(GROUP):
                first = (h * GROUP + r) * HEAD_SIZE
                start = (n * GROUP + r) * steps
                out_ref[n, :, first : first + HEAD_SIZE] = result[start : start + steps, :].astype(
                    jnp.bfloat16
                )


def merge(got, local, local_aux, shape):
    return pl.pallas_call(
        merge_kernel,
        out_shape=jax.ShapeDtypeStruct(shape, jnp.bfloat16),
        in_specs=[whole()] * 3,
        out_specs=whole(),
        compiler_params=LIMIT,
        name="merge",
    )(got, local, local_aux)


def body(
    queries,
    step_keys,
    step_values,
    sample_keys,
    sample_values,
    suffix_len,
    prompt_id,
    document_keys,
    document_values,
):
    owned, steps, _ = queries.shape
    devices = lax.axis_size("seq")
    rows = steps * GROUP
    assert 2 * owned * rows == LANES and devices % KEY_VALUE_HEADS == 0
    arrived = {}

    def exchange(piece, partner):
        route = [(i, i ^ partner) for i in range(devices)]
        arrived[partner] = near(lax.ppermute(piece, "seq", route))

    early = head_slices(document_keys, document_values, EARLY)
    for partner, piece in zip(EARLY, early):
        exchange(piece, partner)
    packed = pack_queries(queries, prompt_id, devices)
    head_queries = lax.all_to_all(packed, "seq", split_axis=0, concat_axis=0, tiled=True)
    late = head_slices(document_keys, document_values, LATE + (0,))
    arrived[0] = near(late[-1])
    for partner, piece in zip(LATE, late):
        exchange(piece, partner)
    head_ids = head_queries[:, owned * rows, :owned].reshape(-1).astype(jnp.int32)
    state = first_stage(
        head_ids, near(head_queries), [arrived[k] for k in (0, 6, 7)], rows
    )
    state = next_stage(state, [arrived[k] for k in (1, 4, 2)])
    sent = last_stage(head_ids, state, [arrived[k] for k in (5, 3)], rows, devices)
    local, local_aux = suffix_part(
        suffix_len, packed, far(sample_keys), far(sample_values), step_keys, step_values
    )
    got = near(lax.all_to_all(sent, "seq", split_axis=0, concat_axis=0, tiled=True))
    return merge(got, near(local), near(local_aux), queries.shape)


def solution(mesh):
    shared = P(("groups", "seq"), None, None)
    split = P("groups", "seq", None)
    return jax.shard_map(
        body,
        mesh=mesh,
        in_specs=(shared,) * 5 + (P(("groups", "seq")),) * 2 + (split,) * 2,
        out_specs=shared,
        check_vma=False,
    )
```

profile of v0, /device:TPU:0, one launch (start us, length us, event | category | flops | bytes accessed | tf_op | source)
XLA Modules:
  0.0 65.8 jit_solution(6201401542406863703)
XLA Ops:
  0.0 1.7 %pack_queries.1.query_ref = bf16[16,80,128]{2,1,0:T(8,128)(2,1)} custom-call(s32[2]{0:T(128)} %ids_ref.1, bf16[2,4,8192]{2,1,0:T(4,128)(2,1)} %queries_ref.1), custom_call_target="tpu_custom_call" | custom-call | tf_op jit(solution)/shard_map/pack_queries/pallas_call | solution.py:91
  1.7 7.4 %all-to-all-start = ((bf16[16,80,128]{2,1,0:T(8,128)(2,1)}), bf16[16,80,128]{2,1,0:T(8,128)(2,1)S(1)}, u32[]{:S(2)}, u32[]{:S(2)}) async-start(bf16[16,80,128]{2,1,0:T(8,128)(2,1)} %pack_queries.1.query_ref), calls=%async_computation | async-start | bytes 655360 | tf_op jit(solution)/shard_map/all_to_all | solution.py:422
  9.1 1.2 %head_slices.3 = (bf16[2,2,256,128]{3,2,1,0:T(8,128)(2,1)S(1)}, bf16[2,2,256,128]{3,2,1,0:T(8,128)(2,1)S(1)}) custom-call(bf16[2,256,1024]{2,1,0:T(8,128)(2,1)} %keys_ref.4, bf16[2,256,1024]{2,1,0:T(8,128)(2,1)} %values_ref.4), custom_call_target="tpu_custom_call" | custom-call | tf_op jit(solution)/shard_map/head_slices/pallas_call | solution.py:56
  10.3 2.9 %collective-permute-start = (bf16[2,2,256,128]{3,2,1,0:T(8,128)(2,1)S(1)}, bf16[2,2,256,128]{3,2,1,0:T(8,128)(2,1)S(1)}, u32[]{:S(2)}, u32[]{:S(2)}) collective-permute-start(bf16[2,2,256,128]{3,2,1,0:T(8,128)(2,1)S(1)} %get-tuple-element.23), channel_id=1, source_target_pairs={{0,6},{1,7},{2,4},{3,5},{4,2},{5,3},{6,0},{7,1},{8,14},{9,15},{10,... | collective-permute-start | bytes 786440 | tf_op jit(solution)/shard_map/ppermute | solution.py:416
  13.1 0.0 collective-permute-start.1
  13.1 2.3 %head_slices.2 = (bf16[2,2,256,128]{3,2,1,0:T(8,128)(2,1)S(1)}, bf16[2,2,256,128]{3,2,1,0:T(8,128)(2,1)S(1)}, bf16[2,2,256,128]{3,2,1,0:T(8,128)(2,1)S(1)}, bf16...) custom-call(bf16[2,256,1024]{2,1,0:T(8,128)(2,1)} %keys_ref.4, ...), custom_call_target="tpu_custom_call" | custom-call | tf_op jit(solution)/shard_map/head_slices/pallas_call | solution.py:56
  15.4 0.0 copy-start
  15.4 0.0 copy-start.1
  15.5 0.0 copy-start.2
  15.5 0.3 collective-permute-start.2
  15.8 1.9 %collective-permute-start.3 = (bf16[2,2,256,128]{3,2,1,0:T(8,128)(2,1)S(1)}, bf16[2,2,256,128]{3,2,1,0:T(8,128)(2,1)S(1)}, u32[]{:S(2)}, u32[]{:S(2)}) collective-permute-start(bf16[2,2,256,128]{3,2,1,0:T(8,128)(2,1)S(1)} %get-tuple-element.30), channel_id=1, source_target_pairs={{0,4},{1,5},{2,6},{3,7},{4,0},{5,1},{6,2},{7,3},{8,12},{9,13},{10,... | collective-permute-start | bytes 786440 | tf_op jit(solution)/shard_map/ppermute | solution.py:416
  17.7 1.5 %collective-permute-start.4 = (bf16[2,2,256,128]{3,2,1,0:T(8,128)(2,1)S(1)}, bf16[2,2,256,128]{3,2,1,0:T(8,128)(2,1)S(1)}, u32[]{:S(2)}, u32[]{:S(2)}) collective-permute-start(bf16[2,2,256,128]{3,2,1,0:T(8,128)(2,1)S(1)} %get-tuple-element.31), channel_id=1, source_target_pairs={{0,2},{1,3},{2,0},{3,1},{4,6},{5,7},{6,4},{7,5},{8,10},{9,11},{10,... | collective-permute-start | bytes 786440 | tf_op jit(solution)/shard_map/ppermute | solution.py:416
  19.1 5.4 %collective-permute-done.refs_1_ = bf16[2,2,256,128]{3,2,1,0:T(8,128)(2,1)S(1)} collective-permute-done((bf16[2,2,256,128]{3,2,1,0:T(8,128)(2,1)S(1)}, bf16[2,2,256,128]{3,2,1,0:T(8,128)(2,1)S(1)}, u32[]{:S(2)}, u32[]{:S(2)}) %collective-permute-start) | collective-permute-done | bytes 262176 | tf_op jit(solution)/shard_map/ppermute | solution.py:416
  24.6 0.0 collective-permute-start.5
  24.6 4.5 %collective-permute-done.1.refs_2_ = bf16[2,2,256,128]{3,2,1,0:T(8,128)(2,1)S(1)} collective-permute-done((bf16[2,2,256,128]{3,2,1,0:T(8,128)(2,1)S(1)}, bf16[2,2,256,128]{3,2,1,0:T(8,128)(2,1)S(1)}, u32[]{:S(2)}, u32[]{:S(2)}) %collective-permute-start.1) | collective-permute-done | bytes 262176 | tf_op jit(solution)/shard_map/ppermute | solution.py:416
  29.0 1.1 %collective-permute-start.6 = (bf16[2,2,256,128]{3,2,1,0:T(8,128)(2,1)S(1)}, bf16[2,2,256,128]{3,2,1,0:T(8,128)(2,1)S(1)}, u32[]{:S(2)}, u32[]{:S(2)}) collective-permute-start(bf16[2,2,256,128]{3,2,1,0:T(8,128)(2,1)S(1)} %get-tuple-element.36), channel_id=1, source_target_pairs={{0,3},{1,2},{2,1},{3,0},{4,7},{5,6},{6,5},{7,4},{8,11},{9,10},{10,... | collective-permute-start | bytes 786440 | tf_op jit(solution)/shard_map/ppermute | solution.py:416
  30.1 0.0 all-to-all-done.queries_ref
  30.2 0.1 reshape.2.ids_ref
  30.3 3.9 %first_stage.1 = (bf16[1024,128]{1,0:T(8,128)(2,1)S(1)}, f32[1024,128]{1,0:T(8,128)S(1)}, f32[1024,128]{1,0:T(8,128)S(1)}, f32[1024,128]{1,0:T(8,128)S(1)}) custom-call(s32[32]{0:T(128)S(1)} %reshape.2.ids_ref, bf16[16,80,128]{2,1,0:T(8,128)(2,1)S(1)} %all-to-all-done.queries_ref, bf16[2,2,256,128]{3,2,1,0:T(8,128)(2,1)S(1)} %get-tuple-element.22.refs_0_, ...), custom_call_target="tpu_custom_call" | custom-call | tf_op jit(solution)/shard_map/first_stage/pallas_call | solution.py:301
  34.1 0.0 collective-permute-done.2.refs_0_
  34.1 0.7 %collective-permute-done.3.refs_1_ = bf16[2,2,256,128]{3,2,1,0:T(8,128)(2,1)S(1)} collective-permute-done((bf16[2,2,256,128]{3,2,1,0:T(8,128)(2,1)S(1)}, bf16[2,2,256,128]{3,2,1,0:T(8,128)(2,1)S(1)}, u32[]{:S(2)}, u32[]{:S(2)}) %collective-permute-start.3) | collective-permute-done | bytes 262176 | tf_op jit(solution)/shard_map/ppermute | solution.py:416
  34.9 0.4 collective-permute-done.4.refs_2_
  35.2 3.1 %next_stage.1 = (f32[1024,128]{1,0:T(8,128)S(1)}, f32[1024,128]{1,0:T(8,128)S(1)}, f32[1024,128]{1,0:T(8,128)S(1)}) custom-call(bf16[1024,128]{1,0:T(8,128)(2,1)S(1)} %get-tuple-element.25.sorted_ref, f32[1024,128]{1,0:T(8,128)S(1)} %get-tuple-element.26.acc_in, f32[1024,128]{1,0:T(8,128)S(1)} %get-tuple-element.27.peak_in, ...), custom_call_target="tpu_custom_call" | custom-call | tf_op jit(solution)/shard_map/next_stage/pallas_call | solution.py:321
  38.3 1.1 %collective-permute-done.5.refs_0_ = bf16[2,2,256,128]{3,2,1,0:T(8,128)(2,1)S(1)} collective-permute-done((bf16[2,2,256,128]{3,2,1,0:T(8,128)(2,1)S(1)}, bf16[2,2,256,128]{3,2,1,0:T(8,128)(2,1)S(1)}, u32[]{:S(2)}, u32[]{:S(2)}) %collective-permute-start.5) | collective-permute-done | bytes 262176 | tf_op jit(solution)/shard_map/ppermute | solution.py:416
  39.5 0.9 %collective-permute-done.6.refs_1_ = bf16[2,2,256,128]{3,2,1,0:T(8,128)(2,1)S(1)} collective-permute-done((bf16[2,2,256,128]{3,2,1,0:T(8,128)(2,1)S(1)}, bf16[2,2,256,128]{3,2,1,0:T(8,128)(2,1)S(1)}, u32[]{:S(2)}, u32[]{:S(2)}) %collective-permute-start.6) | collective-permute-done | bytes 262176 | tf_op jit(solution)/shard_map/ppermute | solution.py:416
  40.4 4.5 %last_stage.1 = f32[16,72,128]{2,1,0:T(8,128)} custom-call(s32[32]{0:T(128)S(1)} %reshape.2.ids_ref, bf16[1024,128]{1,0:T(8,128)(2,1)S(1)} %get-tuple-element.25.sorted_ref, f32[1024,128]{1,0:T(8,128)S(1)} %get-tuple-element.32.acc_ref, f32[1024,128]{1,0:T(8,128)S(1)} %get-tuple-element.33.peak_ref, f32[1024,128]{1,0:T(8,128)S(1)} %get-tuple-element.34.total_ref, ...), custom_call_target="tpu_custom_call" | custom-call | tf_op jit(solution)/shard_map/last_stage/pallas_call | solution.py:337
  44.9 4.3 %all-to-all-start.1 = ((f32[16,72,128]{2,1,0:T(8,128)}), f32[16,72,128]{2,1,0:T(8,128)S(1)}, u32[]{:S(2)}, u32[]{:S(2)}) async-start(f32[16,72,128]{2,1,0:T(8,128)} %last_stage.1), calls=%async_computation.1 | async-start | bytes 1179648 | tf_op jit(solution)/shard_map/all_to_all | solution.py:436
  49.2 0.0 copy-done
  49.2 0.0 copy-done.1
  49.2 9.6 %suffix_part.1 = (f32[8,64,128]{2,1,0:T(8,128)S(1)}, f32[8,1,128]{2,1,0:T(1,128)S(1)}) custom-call(s32[2]{0:T(128)S(1)} %copy-done.2, bf16[16,80,128]{2,1,0:T(8,128)(2,1)} %pack_queries.1.query_ref, bf16[2,1024,1024]{2,1,0:T(8,128)(2,1)} %keys_ref.5, bf16[2,1024,1024]{2,1,0:T(8,128)(2,1)} %values_ref.5, bf16[2,4,1024]{2,1,0:T(4,128)(2,1)S(1)} %copy-done, ...), custom_call_target="tpu_custom_call" | custom-call | tf_op jit(solution)/shard_map/suffix_part/pallas_call | solution.py:155
  58.8 5.7 %all-to-all-done.1.got_ref = f32[16,72,128]{2,1,0:T(8,128)S(1)} async-done(((f32[16,72,128]{2,1,0:T(8,128)}), f32[16,72,128]{2,1,0:T(8,128)S(1)}, u32[]{:S(2)}, u32[]{:S(2)}) %all-to-all-start.1) | async-done | bytes 589856 | tf_op jit(solution)/shard_map/all_to_all | solution.py:436
  64.5 1.2 %merge.1 = bf16[2,4,8192]{2,1,0:T(4,128)(2,1)} custom-call(f32[16,72,128]{2,1,0:T(8,128)S(1)} %all-to-all-done.1.got_ref, f32[8,64,128]{2,1,0:T(8,128)S(1)} %get-tuple-element.37.local_ref, f32[8,1,128]{2,1,0:T(1,128)S(1)} %get-tuple-element.38.local_aux_ref), custom_call_target="tpu_custom_call" | custom-call | tf_op jit(solution)/shard_map/merge/pallas_call | solution.py:387
  (2 shorter events, 0.0 us)
Async XLA Ops:
  1.7 28.5 %all-to-all-start = ((bf16[16,80,128]{2,1,0:T(8,128)(2,1)}), bf16[16,80,128]{2,1,0:T(8,128)(2,1)S(1)}, u32[]{:S(2)}, u32[]{:S(2)}) async-start(bf16[16,80,128]{2,1,0:T(8,128)(2,1)} %pack_queries.1.query_ref), calls=%async_computation | async-start | bytes 655360 | tf_op jit(solution)/shard_map/all_to_all | solution.py:422
  10.3 14.3 %collective-permute-start = (bf16[2,2,256,128]{3,2,1,0:T(8,128)(2,1)S(1)}, bf16[2,2,256,128]{3,2,1,0:T(8,128)(2,1)S(1)}, u32[]{:S(2)}, u32[]{:S(2)}) collective-permute-start(bf16[2,2,256,128]{3,2,1,0:T(8,128)(2,1)S(1)} %get-tuple-element.23), channel_id=1, source_target_pairs={{0,6},{1,7},{2,4},{3,5},{4,2},{5,3},{6,0},{7,1},{8,14},{9,15},{10,... | collective-permute-start | bytes 786440 | tf_op jit(solution)/shard_map/ppermute | solution.py:416
  13.1 15.9 %collective-permute-start.1 = (bf16[2,2,256,128]{3,2,1,0:T(8,128)(2,1)S(1)}, bf16[2,2,256,128]{3,2,1,0:T(8,128)(2,1)S(1)}, u32[]{:S(2)}, u32[]{:S(2)}) collective-permute-start(bf16[2,2,256,128]{3,2,1,0:T(8,128)(2,1)S(1)} %get-tuple-element.24), channel_id=1, source_target_pairs={{0,7},{1,6},{2,5},{3,4},{4,3},{5,2},{6,1},{7,0},{8,15},{9,14},{10,... | collective-permute-start | bytes 786440 | tf_op jit(solution)/shard_map/ppermute | solution.py:416
  15.4 33.7 %copy-start = (bf16[2,4,1024]{2,1,0:T(4,128)(2,1)S(1)}, bf16[2,4,1024]{2,1,0:T(4,128)(2,1)}, u32[]{:S(2)}) copy-start(bf16[2,4,1024]{2,1,0:T(4,128)(2,1)} %new_keys_ref.1) | copy-start | bytes 49156
  15.4 33.7 %copy-start.1 = (bf16[2,4,1024]{2,1,0:T(4,128)(2,1)S(1)}, bf16[2,4,1024]{2,1,0:T(4,128)(2,1)}, u32[]{:S(2)}) copy-start(bf16[2,4,1024]{2,1,0:T(4,128)(2,1)} %new_values_ref.1) | copy-start | bytes 49156
  15.5 33.7 %copy-start.2 = (s32[2]{0:T(128)S(1)}, s32[2]{0:T(128)}, u32[]{:S(2)}) copy-start(s32[2]{0:T(128)} %len_ref.1) | copy-start | bytes 28
  15.5 18.7 %collective-permute-start.2 = (bf16[2,2,256,128]{3,2,1,0:T(8,128)(2,1)}, bf16[2,2,256,128]{3,2,1,0:T(8,128)(2,1)S(1)}, u32[]{:S(2)}, u32[]{:S(2)}) collective-permute-start(bf16[2,2,256,128]{3,2,1,0:T(8,128)(2,1)} %get-tuple-element.29), channel_id=1, source_target_pairs={{0,1},{1,0},{2,3},{3,2},{4,5},{5,4},{6,7},{7,6},{8,9},{9,8},{10,11... | collective-permute-start | bytes 786440 | tf_op jit(solution)/shard_map/ppermute | solution.py:416
  15.8 19.1 %collective-permute-start.3 = (bf16[2,2,256,128]{3,2,1,0:T(8,128)(2,1)S(1)}, bf16[2,2,256,128]{3,2,1,0:T(8,128)(2,1)S(1)}, u32[]{:S(2)}, u32[]{:S(2)}) collective-permute-start(bf16[2,2,256,128]{3,2,1,0:T(8,128)(2,1)S(1)} %get-tuple-element.30), channel_id=1, source_target_pairs={{0,4},{1,5},{2,6},{3,7},{4,0},{5,1},{6,2},{7,3},{8,12},{9,13},{10,... | collective-permute-start | bytes 786440 | tf_op jit(solution)/shard_map/ppermute | solution.py:416
  17.7 17.5 %collective-permute-start.4 = (bf16[2,2,256,128]{3,2,1,0:T(8,128)(2,1)S(1)}, bf16[2,2,256,128]{3,2,1,0:T(8,128)(2,1)S(1)}, u32[]{:S(2)}, u32[]{:S(2)}) collective-permute-start(bf16[2,2,256,128]{3,2,1,0:T(8,128)(2,1)S(1)} %get-tuple-element.31), channel_id=1, source_target_pairs={{0,2},{1,3},{2,0},{3,1},{4,6},{5,7},{6,4},{7,5},{8,10},{9,11},{10,... | collective-permute-start | bytes 786440 | tf_op jit(solution)/shard_map/ppermute | solution.py:416
  24.6 14.9 %collective-permute-start.5 = (bf16[2,2,256,128]{3,2,1,0:T(8,128)(2,1)S(1)}, bf16[2,2,256,128]{3,2,1,0:T(8,128)(2,1)S(1)}, u32[]{:S(2)}, u32[]{:S(2)}) collective-permute-start(bf16[2,2,256,128]{3,2,1,0:T(8,128)(2,1)S(1)} %get-tuple-element.35), channel_id=1, source_target_pairs={{0,5},{1,4},{2,7},{3,6},{4,1},{5,0},{6,3},{7,2},{8,13},{9,12},{10,... | collective-permute-start | bytes 786440 | tf_op jit(solution)/shard_map/ppermute | solution.py:416
  29.0 11.4 %collective-permute-start.6 = (bf16[2,2,256,128]{3,2,1,0:T(8,128)(2,1)S(1)}, bf16[2,2,256,128]{3,2,1,0:T(8,128)(2,1)S(1)}, u32[]{:S(2)}, u32[]{:S(2)}) collective-permute-start(bf16[2,2,256,128]{3,2,1,0:T(8,128)(2,1)S(1)} %get-tuple-element.36), channel_id=1, source_target_pairs={{0,3},{1,2},{2,1},{3,0},{4,7},{5,6},{6,5},{7,4},{8,11},{9,10},{10,... | collective-permute-start | bytes 786440 | tf_op jit(solution)/shard_map/ppermute | solution.py:416
  44.9 19.7 %all-to-all-start.1 = ((f32[16,72,128]{2,1,0:T(8,128)}), f32[16,72,128]{2,1,0:T(8,128)S(1)}, u32[]{:S(2)}, u32[]{:S(2)}) async-start(f32[16,72,128]{2,1,0:T(8,128)} %last_stage.1), calls=%async_computation.1 | async-start | bytes 1179648 | tf_op jit(solution)/shard_map/all_to_all | solution.py:436
where the time goes:
time: 66.3 us; the launch traced here: 65.8 us
  Pallas kernels  27.4 us (41%)
  starting transfers between devices  19.4 us (29%)
  waiting for transfers between devices  18.7 us (28%)
    ppermute x7, waiting for transfers between devices, exchange(): arrived[partner] = near(lax.ppermute(piece, 'seq', route))  13 us
    pallas_call x1, Pallas kernels, suffix_part(): pl.pallas_call(suffix_kernel, grid_spec=pltpu.PrefetchScalarGridSpec(num_...  9.6 us
    ppermute x7, starting transfers between devices, exchange(): arrived[partner] = near(lax.ppermute(piece, 'seq', route))  7.66 us
    all_to_all x1, starting transfers between devices, body(): lax.all_to_all(packed, 'seq', split_axis=0, concat_axis=0, tiled=True)  7.41 us
    all_to_all x1, waiting for transfers between devices, body(): lax.all_to_all(sent, 'seq', split_axis=0, concat_axis=0, tiled=True)  5.73 us
    pallas_call x1, Pallas kernels, last_stage(): pl.pallas_call(functools.partial(last_kernel, rows, min(256, total // pro...  4.46 us
    all_to_all x1, starting transfers between devices, body(): lax.all_to_all(sent, 'seq', split_axis=0, concat_axis=0, tiled=True)  4.3 us
    pallas_call x1, Pallas kernels, first_stage(): pl.pallas_call(functools.partial(first_kernel, rows, min(256, total // pr...  3.87 us
  transfers between devices with their start and end apart: 9, of which 7 were waited for; matrix products, arithmetic and copies ran while one was open for 0% of the time, Pallas kernels for 30%

commit v1 on v0

--- a/solution.py
+++ b/solution.py
@@ -18,6 +18,11 @@
 EARLY = (6, 7)
 LATE = (4, 2, 5, 3, 1)
 LIMIT = pltpu.CompilerParams(vmem_limit_bytes=24 * 1024 * 1024)
+LEVELS = 32767.0
+CODE_STEPS = 256.0
+REST_STEPS = 65000.0
+TINY = 2.0**-120
+AUX_ROWS = 16
 WEIGHT_SCALE = SCALING * math.log2(math.e)
 
 
@@ -113,10 +118,17 @@
     return jnp.sum(jnp.where(mask, columns, 0.0), axis=0, keepdims=True)
 
 
-def max_and_total(peak, total):
-    rows = peak.shape[0]
-    lane = lax.broadcasted_iota(jnp.int32, (rows, LANES), 1)
-    return jnp.where(lane < LANES // 2, peak, total)
+def left_right(left, right):
+    lane = lax.broadcasted_iota(jnp.int32, (left.shape[0], LANES), 1)
+    return jnp.where(lane < LANES // 2, left, right)
+
+
+def to_words(values):
+    return jnp.round(values).astype(jnp.int32).astype(jnp.int16)
+
+
+def from_words(words):
+    return words.astype(jnp.int32).astype(jnp.float32)
 
 
 def suffix_kernel(len_ref, query_ref, keys_ref, values_ref, new_keys_ref, new_values_ref, out_ref, aux_ref):
@@ -144,7 +156,7 @@
             fresh_exp.astype(jnp.bfloat16), new_values_ref[n], ((1,), (0,))
         )
         out_ref[0, n * rows : (n + 1) * rows, :] = out
-        aux_parts.append(max_and_total(peak, total))
+        aux_parts.append(left_right(peak, total))
     aux_ref[0] = diagonal_row(jnp.concatenate(aux_parts, axis=0), diagonal(owned * rows))
 
 
@@ -198,30 +210,20 @@
     return state
 
 
-def find_places(ids_ref, place_ref, count_ref, rows):
-    samples = ids_ref.shape[0]
-    prompts = count_ref.shape[0]
-    per_prompt = samples // prompts
-    for p in range(prompts):
-        count_ref[p] = 0
-
-    def one(sample, carry):
-        prompt = ids_ref[sample]
-        rank = count_ref[prompt]
-        count_ref[prompt] = rank + 1
-        place_ref[sample] = (prompt * per_prompt + rank) * rows
-        return carry
-
-    lax.fori_loop(0, samples, one, 0, unroll=8)
-
-
-def first_kernel(rows, chunk, ids_ref, queries_ref, *refs):
-    pieces, refs = refs[:-6], refs[-6:]
-    sorted_ref, out_ref, peak_ref, total_ref, place_ref, count_ref = refs
+def find_places(ids, prompts, rows):
+    samples = ids.shape[0]
+    order = jnp.arange(samples, dtype=jnp.int32)
+    earlier = (ids[None, :] == ids[:, None]) & (order[None, :] < order[:, None])
+    rank = jnp.sum(earlier.astype(jnp.int32), axis=1)
+    return (ids * (samples // prompts) + rank) * rows
+
+
+def first_kernel(rows, chunk, place_ref, queries_ref, *refs):
+    pieces, refs = refs[:-4], refs[-4:]
+    sorted_ref, out_ref, peak_ref, total_ref = refs
     devices = queries_ref.shape[0]
-    owned = ids_ref.shape[0] // devices
-    prompts = count_ref.shape[0]
-    find_places(ids_ref, place_ref, count_ref, rows)
+    owned = place_ref.shape[0] // devices
+    prompts = pieces[0].shape[1]
 
     def sort_one(device, carry):
         for n in range(owned):
@@ -260,26 +262,30 @@
     lax.fori_loop(0, prompts * chunks, step, 0)
 
 
-def last_kernel(rows, chunk, ids_ref, sorted_ref, acc_ref, peak_ref, total_ref, *refs):
-    pieces, refs = refs[:-5], refs[-5:]
-    out_ref, out_scratch, aux_scratch, place_ref, count_ref = refs
+def last_kernel(rows, chunk, place_ref, sorted_ref, acc_ref, peak_ref, total_ref, *refs):
+    pieces, refs = refs[:-3], refs[-3:]
+    out_ref, out_scratch, aux_scratch = refs
     devices = out_ref.shape[0]
-    owned = ids_ref.shape[0] // devices
-    prompts = count_ref.shape[0]
-    find_places(ids_ref, place_ref, count_ref, rows)
+    owned = place_ref.shape[0] // devices
+    prompts = pieces[0].shape[1]
     chunks = sorted_ref.shape[0] // prompts // chunk
 
     def step(index, carry):
         target = pl.ds(pl.multiple_of(index * chunk, chunk), chunk)
         state = (peak_ref[target, :], total_ref[target, :], acc_ref[target, :])
         peak, total, out = attend(sorted_ref[target, :], pieces, index // chunks, state)
-        out_scratch[target, :] = out
-        aux_scratch[target, :] = max_and_total(peak, total)
+        out = out / total
+        largest = jnp.max(jnp.abs(out), axis=1, keepdims=True)
+        code = jnp.ceil(jnp.log2(jnp.maximum(largest, TINY)) * CODE_STEPS)
+        out = out * (LEVELS * jnp.exp2(code * (-1.0 / CODE_STEPS)))
+        out_scratch[target, :] = to_words(jnp.clip(out, -LEVELS, LEVELS))
+        aux_scratch[target, :] = left_right(peak + jnp.log(total), code)
         return carry
 
     lax.fori_loop(0, prompts * chunks, step, 0)
 
     mask = diagonal(owned * rows)
+    first_rows = lax.broadcasted_iota(jnp.int32, (AUX_ROWS, LANES), 0) < AUX_ROWS // 2
 
     def emit(device, carry):
         aux_parts = []
@@ -288,16 +294,18 @@
             out_ref[device, n * rows : (n + 1) * rows, :] = out_scratch[source, :]
             aux_parts.append(aux_scratch[source, :])
         row = diagonal_row(jnp.concatenate(aux_parts, axis=0), mask)
-        out_ref[device, owned * rows :, :] = jnp.broadcast_to(row, (8, LANES))
+        near_part = jnp.round(row)
+        rest = (row - near_part) * REST_STEPS
+        words = jnp.where(first_rows, near_part, rest)
+        out_ref[device, owned * rows :, :] = to_words(words)
         return carry
 
     lax.fori_loop(0, devices, emit, 0, unroll=4)
 
 
-def first_stage(ids, queries, pieces, rows):
-    samples = ids.shape[0]
-    prompts = pieces[0].shape[1]
-    total = samples * rows
+def first_stage(places, queries, pieces, rows):
+    prompts = pieces[0].shape[1]
+    total = places.shape[0] * rows
     results = pl.pallas_call(
         functools.partial(first_kernel, rows, min(256, total // prompts)),
         out_shape=[
@@ -308,10 +316,9 @@
         ],
         in_specs=[whole(pltpu.SMEM)] + [whole()] * (1 + len(pieces)),
         out_specs=[whole()] * 4,
-        scratch_shapes=[pltpu.SMEM((samples,), jnp.int32), pltpu.SMEM((prompts,), jnp.int32)],
         compiler_params=LIMIT,
         name="first_stage",
-    )(ids, queries, *pieces)
+    )(places, queries, *pieces)
     return [near(result) for result in results]
 
 
@@ -329,26 +336,21 @@
     return [state[0]] + [near(result) for result in results]
 
 
-def last_stage(ids, state, pieces, rows, devices):
-    samples = ids.shape[0]
-    prompts = pieces[0].shape[1]
-    total = samples * rows
-    return (
-        pl.pallas_call(
-            functools.partial(last_kernel, rows, min(256, total // prompts)),
-            out_shape=jax.ShapeDtypeStruct((devices, total // devices + 8, HEAD_SIZE), jnp.float32),
-            in_specs=[whole(pltpu.SMEM)] + [whole()] * (4 + len(pieces)),
-            out_specs=whole(),
-            scratch_shapes=[
-                pltpu.VMEM((total, HEAD_SIZE), jnp.float32),
-                pltpu.VMEM((total, HEAD_SIZE), jnp.float32),
-                pltpu.SMEM((samples,), jnp.int32),
-                pltpu.SMEM((prompts,), jnp.int32),
-            ],
-            compiler_params=LIMIT,
-            name="last_stage",
-        )(ids, *state, *pieces)
-    )
+def last_stage(places, state, pieces, rows, devices):
+    prompts = pieces[0].shape[1]
+    total = places.shape[0] * rows
+    return pl.pallas_call(
+        functools.partial(last_kernel, rows, min(256, total // prompts)),
+        out_shape=jax.ShapeDtypeStruct((devices, total // devices + AUX_ROWS, HEAD_SIZE), jnp.int16),
+        in_specs=[whole(pltpu.SMEM)] + [whole()] * (4 + len(pieces)),
+        out_specs=whole(),
+        scratch_shapes=[
+            pltpu.VMEM((total, HEAD_SIZE), jnp.int16),
+            pltpu.VMEM((total, HEAD_SIZE), jnp.float32),
+        ],
+        compiler_params=LIMIT,
+        name="last_stage",
+    )(places, *state, *pieces)
 
 
 def merge_kernel(got_ref, local_ref, local_aux_ref, out_ref):
@@ -356,24 +358,28 @@
     rows = local_ref.shape[1]
     half = LANES // 2
     groups = got_ref.shape[0] // KEY_VALUE_HEADS
-    aux = [local_aux_ref[:, 0, :]]
+    local_aux = local_aux_ref[:, 0, :]
+    local_total = local_aux[:, half:]
+    levels = [local_aux[:, :half] + jnp.log(local_total)]
+    scales = [1.0 / local_total]
     for g in range(groups):
-        aux.append(
-            jnp.concatenate(
-                [got_ref[g * KEY_VALUE_HEADS + h, rows : rows + 1, :] for h in range(KEY_VALUE_HEADS)],
-                axis=0,
-            )
-        )
-    peaks = [a[:, :half] for a in aux]
-    totals = [a[:, half:] for a in aux]
-    highest = functools.reduce(jnp.maximum, peaks)
-    scales = [jnp.exp(peak - highest) for peak in peaks]
-    denominator = functools.reduce(jnp.add, [t * s for t, s in zip(totals, scales)])
-    factors = [jnp.transpose(s / denominator) for s in scales]
+        both = []
+        for h in range(KEY_VALUE_HEADS):
+            words = from_words(got_ref[g * KEY_VALUE_HEADS + h, rows:, :])
+            middle = AUX_ROWS // 2
+            both.append(words[:1] + words[middle : middle + 1] * (1.0 / REST_STEPS))
+        aux = jnp.concatenate(both, axis=0)
+        levels.append(aux[:, :half])
+        scales.append(jnp.exp2(aux[:, half:] * (1.0 / CODE_STEPS)) * (1.0 / LEVELS))
+    highest = functools.reduce(jnp.maximum, levels)
+    weights = [jnp.exp(level - highest) for level in levels]
+    denominator = functools.reduce(jnp.add, weights)
+    factors = [jnp.transpose(w * s / denominator) for w, s in zip(weights, scales)]
     for h in range(KEY_VALUE_HEADS):
         result = local_ref[h] * factors[0][:, h : h + 1]
         for g in range(groups):
-            result += got_ref[g * KEY_VALUE_HEADS + h, :rows, :] * factors[g + 1][:, h : h + 1]
+            part = from_words(got_ref[g * KEY_VALUE_HEADS + h, :rows, :])
+            result += part * factors[g + 1][:, h : h + 1]
         for n in range(owned):
             for r in range(GROUP):
                 first = (h * GROUP + r) * HEAD_SIZE
@@ -415,21 +421,19 @@
         route = [(i, i ^ partner) for i in range(devices)]
         arrived[partner] = near(lax.ppermute(piece, "seq", route))
 
-    early = head_slices(document_keys, document_values, EARLY)
-    for partner, piece in zip(EARLY, early):
+    slices = head_slices(document_keys, document_values, EARLY + LATE + (0,))
+    for partner, piece in zip(EARLY, slices):
         exchange(piece, partner)
     packed = pack_queries(queries, prompt_id, devices)
     head_queries = lax.all_to_all(packed, "seq", split_axis=0, concat_axis=0, tiled=True)
-    late = head_slices(document_keys, document_values, LATE + (0,))
-    arrived[0] = near(late[-1])
-    for partner, piece in zip(LATE, late):
+    arrived[0] = near(slices[-1])
+    for partner, piece in zip(LATE, slices[len(EARLY) :]):
         exchange(piece, partner)
     head_ids = head_queries[:, owned * rows, :owned].reshape(-1).astype(jnp.int32)
-    state = first_stage(
-        head_ids, near(head_queries), [arrived[k] for k in (0, 6, 7)], rows
-    )
+    places = find_places(head_ids, document_keys.shape[0], rows)
+    state = first_stage(places, near(head_queries), [arrived[k] for k in (0, 6, 7)], rows)
     state = next_stage(state, [arrived[k] for k in (1, 4, 2)])
-    sent = last_stage(head_ids, state, [arrived[k] for k in (5, 3)], rows, devices)
+    sent = last_stage(places, state, [arrived[k] for k in (5, 3)], rows, devices)
     local, local_aux = suffix_part(
         suffix_len, packed, far(sample_keys), far(sample_values), step_keys, step_values
     )

time: 66.3 us -> 62.9 us (0.949)
  waiting for transfers between devices: 18.7 us -> 15.6 us
  Pallas kernels: 27.4 us -> 26.4 us
    all_to_all x1, waiting for transfers between devices: 5.73 us -> 1.43 us  [body(): lax.all_to_all(sent, 'seq', split_axis=0, concat_axis=0, tiled=True)]
    all_to_all x1, waiting for transfers between devices: 0.01 us -> 2.59 us  [body(): lax.all_to_all(packed, 'seq', split_axis=0, concat_axis=0, tiled=True)]
    ppermute x7, waiting for transfers between devices: 13 us -> 11.6 us  [exchange(): arrived[partner] = near(lax.ppermute(piece, 'seq', route))]
    pallas_call x2 -> x1, Pallas kernels: 3.43 us -> 2.51 us  [head_slices(): pl.pallas_call(functools.partial(slice_kernel, partners), out_shape=[piec...]
    all_to_all x1, starting transfers between devices: 4.3 us -> 5.1 us  [body(): lax.all_to_all(sent, 'seq', split_axis=0, concat_axis=0, tiled=True)]
  transfers between devices with their start and end apart: 9 -> 9, of which waited for: 7 -> 8; matrix products, arithmetic and copies ran while one was open for 0% -> 0% of each run, Pallas kernels for 30% -> 30%
where the time goes in v1:
time: 62.9 us; the launch traced here: 62.4 us
  Pallas kernels  26.4 us (42%)
  starting transfers between devices  20 us (32%)
  waiting for transfers between devices  15.6 us (25%)
    ppermute x7, waiting for transfers between devices, exchange(): arrived[partner] = near(lax.ppermute(piece, 'seq', route))  11.6 us
    pallas_call x1, Pallas kernels, suffix_part(): pl.pallas_call(suffix_kernel, grid_spec=pltpu.PrefetchScalarGridSpec(num_...  9.6 us
    ppermute x7, starting transfers between devices, exchange(): arrived[partner] = near(lax.ppermute(piece, 'seq', route))  7.48 us
    all_to_all x1, starting transfers between devices, body(): lax.all_to_all(packed, 'seq', split_axis=0, concat_axis=0, tiled=True)  7.41 us
    all_to_all x1, starting transfers between devices, body(): lax.all_to_all(sent, 'seq', split_axis=0, concat_axis=0, tiled=True)  5.1 us
    pallas_call x1, Pallas kernels, last_stage(): pl.pallas_call(functools.partial(last_kernel, rows, min(256, total // pro...  4.62 us
    pallas_call x1, Pallas kernels, first_stage(): pl.pallas_call(functools.partial(first_kernel, rows, min(256, total // pr...  3.71 us
    pallas_call x1, Pallas kernels, next_stage(): pl.pallas_call(functools.partial(next_kernel, min(256, total // prompts))...  3.13 us
  transfers between devices with their start and end apart: 9, of which 8 were waited for; matrix products, arithmetic and copies ran while one was open for 0% of the time, Pallas kernels for 30%

profile of v1, /device:TPU:0, one launch (start us, length us, event | category | flops | bytes accessed | tf_op | source)
XLA Modules:
  0.0 62.4 jit_solution(17027773915223869503)
XLA Ops:
  0.0 1.7 %pack_queries.1.query_ref = bf16[16,80,128]{2,1,0:T(8,128)(2,1)} custom-call(s32[2]{0:T(128)} %ids_ref.1, bf16[2,4,8192]{2,1,0:T(4,128)(2,1)} %queries_ref.1), custom_call_target="tpu_custom_call" | custom-call | tf_op jit(solution)/shard_map/pack_queries/pallas_call | solution.py:96
  1.7 7.4 %all-to-all-start = ((bf16[16,80,128]{2,1,0:T(8,128)(2,1)}), bf16[16,80,128]{2,1,0:T(8,128)(2,1)S(1)}, u32[]{:S(2)}, u32[]{:S(2)}) async-start(bf16[16,80,128]{2,1,0:T(8,128)(2,1)} %pack_queries.1.query_ref), calls=%async_computation | async-start | bytes 655360 | tf_op jit(solution)/shard_map/all_to_all | solution.py:428
  9.1 0.0 copy-start
  9.1 0.0 copy-start.1
  9.1 0.0 copy-start.2
  9.1 2.5 %head_slices.1 = (bf16[2,2,256,128]{3,2,1,0:T(8,128)(2,1)}, bf16[2,2,256,128]{3,2,1,0:T(8,128)(2,1)S(1)}, bf16[2,2,256,128]{3,2,1,0:T(8,128)(2,1)S(1)}, bf16[2,2...) custom-call(bf16[2,256,1024]{2,1,0:T(8,128)(2,1)} %keys_ref.2, ...), custom_call_target="tpu_custom_call" | custom-call | tf_op jit(solution)/shard_map/head_slices/pallas_call | solution.py:61
  11.7 2.9 %collective-permute-start = (bf16[2,2,256,128]{3,2,1,0:T(8,128)(2,1)}, bf16[2,2,256,128]{3,2,1,0:T(8,128)(2,1)S(1)}, u32[]{:S(2)}, u32[]{:S(2)}) collective-permute-start(bf16[2,2,256,128]{3,2,1,0:T(8,128)(2,1)} %get-tuple-element.23), channel_id=1, source_target_pairs={{0,6},{1,7},{2,4},{3,5},{4,2},{5,3},{6,0},{7,1},{8,14},{9,15},{10,... | collective-permute-start | bytes 786440 | tf_op jit(solution)/shard_map/ppermute | solution.py:422
  14.5 0.0 collective-permute-start.1
  14.5 0.2 collective-permute-start.2
  14.8 1.9 %collective-permute-start.3 = (bf16[2,2,256,128]{3,2,1,0:T(8,128)(2,1)S(1)}, bf16[2,2,256,128]{3,2,1,0:T(8,128)(2,1)S(1)}, u32[]{:S(2)}, u32[]{:S(2)}) collective-permute-start(bf16[2,2,256,128]{3,2,1,0:T(8,128)(2,1)S(1)} %get-tuple-element.30), channel_id=1, source_target_pairs={{0,4},{1,5},{2,6},{3,7},{4,0},{5,1},{6,2},{7,3},{8,12},{9,13},{10,... | collective-permute-start | bytes 786440 | tf_op jit(solution)/shard_map/ppermute | solution.py:422
  16.7 1.5 %collective-permute-start.4 = (bf16[2,2,256,128]{3,2,1,0:T(8,128)(2,1)S(1)}, bf16[2,2,256,128]{3,2,1,0:T(8,128)(2,1)S(1)}, u32[]{:S(2)}, u32[]{:S(2)}) collective-permute-start(bf16[2,2,256,128]{3,2,1,0:T(8,128)(2,1)S(1)} %get-tuple-element.31), channel_id=1, source_target_pairs={{0,2},{1,3},{2,0},{3,1},{4,6},{5,7},{6,4},{7,5},{8,10},{9,11},{10,... | collective-permute-start | bytes 786440 | tf_op jit(solution)/shard_map/ppermute | solution.py:422
  18.1 2.6 %all-to-all-done.queries_ref = bf16[16,80,128]{2,1,0:T(8,128)(2,1)S(1)} async-done(((bf16[16,80,128]{2,1,0:T(8,128)(2,1)}), bf16[16,80,128]{2,1,0:T(8,128)(2,1)S(1)}, u32[]{:S(2)}, u32[]{:S(2)}) %all-to-all-start) | async-done | bytes 327712 | tf_op jit(solution)/shard_map/all_to_all | solution.py:428
  20.8 0.1 reshape.12
  20.9 3.4 %collective-permute-done.refs_1_ = bf16[2,2,256,128]{3,2,1,0:T(8,128)(2,1)S(1)} collective-permute-done((bf16[2,2,256,128]{3,2,1,0:T(8,128)(2,1)}, bf16[2,2,256,128]{3,2,1,0:T(8,128)(2,1)S(1)}, u32[]{:S(2)}, u32[]{:S(2)}) %collective-permute-start) | collective-permute-done | bytes 262176 | tf_op jit(solution)/shard_map/ppermute | solution.py:422
  24.2 0.1 collective-permute-start.5
  24.4 4.9 %collective-permute-done.1.refs_2_ = bf16[2,2,256,128]{3,2,1,0:T(8,128)(2,1)S(1)} collective-permute-done((bf16[2,2,256,128]{3,2,1,0:T(8,128)(2,1)S(1)}, bf16[2,2,256,128]{3,2,1,0:T(8,128)(2,1)S(1)}, u32[]{:S(2)}, u32[]{:S(2)}) %collective-permute-start.1) | collective-permute-done | bytes 262176 | tf_op jit(solution)/shard_map/ppermute | solution.py:422
  29.3 0.8 %collective-permute-start.6 = (bf16[2,2,256,128]{3,2,1,0:T(8,128)(2,1)S(1)}, bf16[2,2,256,128]{3,2,1,0:T(8,128)(2,1)S(1)}, u32[]{:S(2)}, u32[]{:S(2)}) collective-permute-start(bf16[2,2,256,128]{3,2,1,0:T(8,128)(2,1)S(1)} %get-tuple-element.36), channel_id=1, source_target_pairs={{0,3},{1,2},{2,1},{3,0},{4,7},{5,6},{6,5},{7,4},{8,11},{9,10},{10,... | collective-permute-start | bytes 786440 | tf_op jit(solution)/shard_map/ppermute | solution.py:422
  30.2 0.2 convert_reduce_fusion
  30.4 3.7 %first_stage.1 = (bf16[1024,128]{1,0:T(8,128)(2,1)S(1)}, f32[1024,128]{1,0:T(8,128)S(1)}, f32[1024,128]{1,0:T(8,128)S(1)}, f32[1024,128]{1,0:T(8,128)S(1)}) custom-call(s32[32]{0:T(128)S(1)} %add_multiply_fusion.place_ref, bf16[16,80,128]{2,1,0:T(8,128)(2,1)S(1)} %all-to-all-done.queries_ref, bf16[2,2,256,128]{3,2,1,0:T(8,128)(2,1)S(1)} %get-tuple-element.22.refs_0_, ...), custom_call_target="tpu_custom_call" | custom-call | tf_op jit(solution)/shard_map/first_stage/pallas_call | solution.py:309
  34.1 0.0 collective-permute-done.2.refs_0_
  34.1 0.8 %collective-permute-done.3.refs_1_ = bf16[2,2,256,128]{3,2,1,0:T(8,128)(2,1)S(1)} collective-permute-done((bf16[2,2,256,128]{3,2,1,0:T(8,128)(2,1)S(1)}, bf16[2,2,256,128]{3,2,1,0:T(8,128)(2,1)S(1)}, u32[]{:S(2)}, u32[]{:S(2)}) %collective-permute-start.3) | collective-permute-done | bytes 262176 | tf_op jit(solution)/shard_map/ppermute | solution.py:422
  34.9 0.2 collective-permute-done.4.refs_2_
  35.1 3.1 %next_stage.1 = (f32[1024,128]{1,0:T(8,128)S(1)}, f32[1024,128]{1,0:T(8,128)S(1)}, f32[1024,128]{1,0:T(8,128)S(1)}) custom-call(bf16[1024,128]{1,0:T(8,128)(2,1)S(1)} %get-tuple-element.25.sorted_ref, f32[1024,128]{1,0:T(8,128)S(1)} %get-tuple-element.26.acc_in, f32[1024,128]{1,0:T(8,128)S(1)} %get-tuple-element.27.peak_in, ...), custom_call_target="tpu_custom_call" | custom-call | tf_op jit(solution)/shard_map/next_stage/pallas_call | solution.py:328
  38.2 1.7 %collective-permute-done.5.refs_0_ = bf16[2,2,256,128]{3,2,1,0:T(8,128)(2,1)S(1)} collective-permute-done((bf16[2,2,256,128]{3,2,1,0:T(8,128)(2,1)S(1)}, bf16[2,2,256,128]{3,2,1,0:T(8,128)(2,1)S(1)}, u32[]{:S(2)}, u32[]{:S(2)}) %collective-permute-start.5) | collective-permute-done | bytes 262176 | tf_op jit(solution)/shard_map/ppermute | solution.py:422
  40.0 0.5 collective-permute-done.6.refs_1_
  40.5 4.6 %last_stage.1 = s16[16,80,128]{2,1,0:T(8,128)(2,1)} custom-call(s32[32]{0:T(128)S(1)} %add_multiply_fusion.place_ref, bf16[1024,128]{1,0:T(8,128)(2,1)S(1)} %get-tuple-element.25.sorted_ref, f32[1024,128]{1,0:T(8,128)S(1)} %get-tuple-element.32.acc_ref, f32[1024,128]{1,0:T(8,128)S(1)} %get-tuple-element.33.peak_ref, ...), custom_call_target="tpu_custom_call" | custom-call | tf_op jit(solution)/shard_map/last_stage/pallas_call | solution.py:342
  45.1 5.1 %all-to-all-start.1 = ((s16[16,80,128]{2,1,0:T(8,128)(2,1)}), s16[16,80,128]{2,1,0:T(8,128)(2,1)S(1)}, u32[]{:S(2)}, u32[]{:S(2)}) async-start(s16[16,80,128]{2,1,0:T(8,128)(2,1)} %last_stage.1), calls=%async_computation.1 | async-start | bytes 655360 | tf_op jit(solution)/shard_map/all_to_all | solution.py:440
  50.2 0.0 copy-done
  50.2 0.0 copy-done.1
  50.3 9.6 %suffix_part.1 = (f32[8,64,128]{2,1,0:T(8,128)S(1)}, f32[8,1,128]{2,1,0:T(1,128)S(1)}) custom-call(s32[2]{0:T(128)S(1)} %copy-done.2, bf16[16,80,128]{2,1,0:T(8,128)(2,1)} %pack_queries.1.query_ref, bf16[2,1024,1024]{2,1,0:T(8,128)(2,1)} %keys_ref.3, bf16[2,1024,1024]{2,1,0:T(8,128)(2,1)} %values_ref.3, bf16[2,4,1024]{2,1,0:T(4,128)(2,1)S(1)} %copy-done, ...), custom_call_target="tpu_custom_call" | custom-call | tf_op jit(solution)/shard_map/suffix_part/pallas_call | solution.py:167
  59.9 1.4 %all-to-all-done.1.got_ref = s16[16,80,128]{2,1,0:T(8,128)(2,1)S(1)} async-done(((s16[16,80,128]{2,1,0:T(8,128)(2,1)}), s16[16,80,128]{2,1,0:T(8,128)(2,1)S(1)}, u32[]{:S(2)}, u32[]{:S(2)}) %all-to-all-start.1) | async-done | bytes 327712 | tf_op jit(solution)/shard_map/all_to_all | solution.py:440
  61.3 1.1 %merge.1 = bf16[2,4,8192]{2,1,0:T(4,128)(2,1)} custom-call(s16[16,80,128]{2,1,0:T(8,128)(2,1)S(1)} %all-to-all-done.1.got_ref, f32[8,64,128]{2,1,0:T(8,128)S(1)} %get-tuple-element.37.local_ref, f32[8,1,128]{2,1,0:T(1,128)S(1)} %get-tuple-element.38.local_aux_ref), custom_call_target="tpu_custom_call" | custom-call | tf_op jit(solution)/shard_map/merge/pallas_call | solution.py:393
  (3 shorter events, 0.0 us)
Async XLA Ops:
  1.7 19.1 %all-to-all-start = ((bf16[16,80,128]{2,1,0:T(8,128)(2,1)}), bf16[16,80,128]{2,1,0:T(8,128)(2,1)S(1)}, u32[]{:S(2)}, u32[]{:S(2)}) async-start(bf16[16,80,128]{2,1,0:T(8,128)(2,1)} %pack_queries.1.query_ref), calls=%async_computation | async-start | bytes 655360 | tf_op jit(solution)/shard_map/all_to_all | solution.py:428
  9.1 41.1 %copy-start = (bf16[2,4,1024]{2,1,0:T(4,128)(2,1)S(1)}, bf16[2,4,1024]{2,1,0:T(4,128)(2,1)}, u32[]{:S(2)}) copy-start(bf16[2,4,1024]{2,1,0:T(4,128)(2,1)} %new_keys_ref.1) | copy-start | bytes 49156
  9.1 41.1 %copy-start.1 = (bf16[2,4,1024]{2,1,0:T(4,128)(2,1)S(1)}, bf16[2,4,1024]{2,1,0:T(4,128)(2,1)}, u32[]{:S(2)}) copy-start(bf16[2,4,1024]{2,1,0:T(4,128)(2,1)} %new_values_ref.1) | copy-start | bytes 49156
  9.1 41.1 %copy-start.2 = (s32[2]{0:T(128)S(1)}, s32[2]{0:T(128)}, u32[]{:S(2)}) copy-start(s32[2]{0:T(128)} %len_ref.1) | copy-start | bytes 28
  11.7 12.6 %collective-permute-start = (bf16[2,2,256,128]{3,2,1,0:T(8,128)(2,1)}, bf16[2,2,256,128]{3,2,1,0:T(8,128)(2,1)S(1)}, u32[]{:S(2)}, u32[]{:S(2)}) collective-permute-start(bf16[2,2,256,128]{3,2,1,0:T(8,128)(2,1)} %get-tuple-element.23), channel_id=1, source_target_pairs={{0,6},{1,7},{2,4},{3,5},{4,2},{5,3},{6,0},{7,1},{8,14},{9,15},{10,... | collective-permute-start | bytes 786440 | tf_op jit(solution)/shard_map/ppermute | solution.py:422
  14.5 14.8 %collective-permute-start.1 = (bf16[2,2,256,128]{3,2,1,0:T(8,128)(2,1)S(1)}, bf16[2,2,256,128]{3,2,1,0:T(8,128)(2,1)S(1)}, u32[]{:S(2)}, u32[]{:S(2)}) collective-permute-start(bf16[2,2,256,128]{3,2,1,0:T(8,128)(2,1)S(1)} %get-tuple-element.24), channel_id=1, source_target_pairs={{0,7},{1,6},{2,5},{3,4},{4,3},{5,2},{6,1},{7,0},{8,15},{9,14},{10,... | collective-permute-start | bytes 786440 | tf_op jit(solution)/shard_map/ppermute | solution.py:422
  14.5 19.5 %collective-permute-start.2 = (bf16[2,2,256,128]{3,2,1,0:T(8,128)(2,1)S(1)}, bf16[2,2,256,128]{3,2,1,0:T(8,128)(2,1)S(1)}, u32[]{:S(2)}, u32[]{:S(2)}) collective-permute-start(bf16[2,2,256,128]{3,2,1,0:T(8,128)(2,1)S(1)} %get-tuple-element.29), channel_id=1, source_target_pairs={{0,1},{1,0},{2,3},{3,2},{4,5},{5,4},{6,7},{7,6},{8,9},{9,8},{10,11... | collective-permute-start | bytes 786440 | tf_op jit(solution)/shard_map/ppermute | solution.py:422
  14.8 20.1 %collective-permute-start.3 = (bf16[2,2,256,128]{3,2,1,0:T(8,128)(2,1)S(1)}, bf16[2,2,256,128]{3,2,1,0:T(8,128)(2,1)S(1)}, u32[]{:S(2)}, u32[]{:S(2)}) collective-permute-start(bf16[2,2,256,128]{3,2,1,0:T(8,128)(2,1)S(1)} %get-tuple-element.30), channel_id=1, source_target_pairs={{0,4},{1,5},{2,6},{3,7},{4,0},{5,1},{6,2},{7,3},{8,12},{9,13},{10,... | collective-permute-start | bytes 786440 | tf_op jit(solution)/shard_map/ppermute | solution.py:422
  16.7 18.4 %collective-permute-start.4 = (bf16[2,2,256,128]{3,2,1,0:T(8,128)(2,1)S(1)}, bf16[2,2,256,128]{3,2,1,0:T(8,128)(2,1)S(1)}, u32[]{:S(2)}, u32[]{:S(2)}) collective-permute-start(bf16[2,2,256,128]{3,2,1,0:T(8,128)(2,1)S(1)} %get-tuple-element.31), channel_id=1, source_target_pairs={{0,2},{1,3},{2,0},{3,1},{4,6},{5,7},{6,4},{7,5},{8,10},{9,11},{10,... | collective-permute-start | bytes 786440 | tf_op jit(solution)/shard_map/ppermute | solution.py:422
  24.2 15.7 %collective-permute-start.5 = (bf16[2,2,256,128]{3,2,1,0:T(8,128)(2,1)S(1)}, bf16[2,2,256,128]{3,2,1,0:T(8,128)(2,1)S(1)}, u32[]{:S(2)}, u32[]{:S(2)}) collective-permute-start(bf16[2,2,256,128]{3,2,1,0:T(8,128)(2,1)S(1)} %get-tuple-element.35), channel_id=1, source_target_pairs={{0,5},{1,4},{2,7},{3,6},{4,1},{5,0},{6,3},{7,2},{8,13},{9,12},{10,... | collective-permute-start | bytes 786440 | tf_op jit(solution)/shard_map/ppermute | solution.py:422
  29.3 11.2 %collective-permute-start.6 = (bf16[2,2,256,128]{3,2,1,0:T(8,128)(2,1)S(1)}, bf16[2,2,256,128]{3,2,1,0:T(8,128)(2,1)S(1)}, u32[]{:S(2)}, u32[]{:S(2)}) collective-permute-start(bf16[2,2,256,128]{3,2,1,0:T(8,128)(2,1)S(1)} %get-tuple-element.36), channel_id=1, source_target_pairs={{0,3},{1,2},{2,1},{3,0},{4,7},{5,6},{6,5},{7,4},{8,11},{9,10},{10,... | collective-permute-start | bytes 786440 | tf_op jit(solution)/shard_map/ppermute | solution.py:422
  45.1 16.2 %all-to-all-start.1 = ((s16[16,80,128]{2,1,0:T(8,128)(2,1)}), s16[16,80,128]{2,1,0:T(8,128)(2,1)S(1)}, u32[]{:S(2)}, u32[]{:S(2)}) async-start(s16[16,80,128]{2,1,0:T(8,128)(2,1)} %last_stage.1), calls=%async_computation.1 | async-start | bytes 655360 | tf_op jit(solution)/shard_map/all_to_all | solution.py:440

commit v2 on v1

--- a/solution.py
+++ b/solution.py
@@ -15,14 +15,15 @@
 GROUP = QUERY_HEADS // KEY_VALUE_HEADS
 SCALING = HEAD_SIZE ** (-0.5)
 LANES = 128
-EARLY = (6, 7)
-LATE = (4, 2, 5, 3, 1)
+FIRST = (6,)
+EARLY = (7, 4)
+LATE = (5, 2, 3, 1)
 LIMIT = pltpu.CompilerParams(vmem_limit_bytes=24 * 1024 * 1024)
 LEVELS = 32767.0
 CODE_STEPS = 256.0
 REST_STEPS = 65000.0
 TINY = 2.0**-120
-AUX_ROWS = 16
+AUX_ROWS = 8
 WEIGHT_SCALE = SCALING * math.log2(math.e)
 
 
@@ -38,8 +39,7 @@
     return pltpu.with_memory_space_constraint(array, pltpu.HBM)
 
 
-def slice_kernel(partners, keys_ref, values_ref, *refs):
-    out_refs, sem = refs[:-1], refs[-1]
+def start_slices(partners, keys_ref, values_ref, out_refs, sem):
     mine = lax.axis_index("seq") % KEY_VALUE_HEADS
     copies = []
     for slot, partner in enumerate(partners):
@@ -51,7 +51,11 @@
             )
             copy.start()
             copies.append(copy)
-    for copy in copies:
+    return copies
+
+
+def slice_kernel(partners, keys_ref, values_ref, *refs):
+    for copy in start_slices(partners, keys_ref, values_ref, refs[:-1], refs[-1]):
         copy.wait()
 
 
@@ -70,7 +74,7 @@
     return pieces
 
 
-def pack_kernel(ids_ref, queries_ref, out_ref):
+def pack_rows(ids_ref, queries_ref, out_ref):
     owned, steps, _ = queries_ref.shape
     rows = owned * steps * GROUP
     lane = lax.broadcasted_iota(jnp.int32, (out_ref.shape[1] - rows, LANES), 1)
@@ -90,18 +94,37 @@
             out_ref[copy * KEY_VALUE_HEADS + head, rows:, :] = marks
 
 
-def pack_queries(queries, prompt_id, device_count):
+def slice_and_pack_kernel(partners, keys_ref, values_ref, ids_ref, queries_ref, *refs):
+    out_refs, packed_ref, query_buffer, sem, query_sem = refs[:-4], *refs[-4:]
+    load = pltpu.make_async_copy(queries_ref, query_buffer, query_sem)
+    load.start()
+    copies = start_slices(partners, keys_ref, values_ref, out_refs, sem)
+    load.wait()
+    pack_rows(ids_ref, query_buffer, packed_ref)
+    for copy in copies:
+        copy.wait()
+
+
+def slices_and_queries(keys, values, partners, queries, prompt_id, devices):
+    prompts, block, _ = keys.shape
     owned, steps, _ = queries.shape
-    rows = owned * steps * GROUP
-    packed = pl.pallas_call(
-        pack_kernel,
-        out_shape=jax.ShapeDtypeStruct((device_count, rows + 16, HEAD_SIZE), jnp.bfloat16),
-        in_specs=[whole(pltpu.SMEM), whole()],
-        out_specs=whole(),
-        compiler_params=LIMIT,
-        name="pack_queries",
-    )(far(prompt_id), far(queries))
-    return packed
+    piece = jax.ShapeDtypeStruct((2, prompts, block, HEAD_SIZE), keys.dtype)
+    rows = owned * steps * GROUP + AUX_ROWS
+    results = pl.pallas_call(
+        functools.partial(slice_and_pack_kernel, partners),
+        out_shape=[piece] * len(partners)
+        + [jax.ShapeDtypeStruct((devices, rows, HEAD_SIZE), jnp.bfloat16)],
+        in_specs=[whole(pltpu.HBM)] * 2 + [whole(pltpu.SMEM), whole(pltpu.HBM)],
+        out_specs=[whole()] * (len(partners) + 1),
+        scratch_shapes=[
+            pltpu.VMEM(queries.shape, queries.dtype),
+            pltpu.SemaphoreType.DMA((len(partners), 2)),
+            pltpu.SemaphoreType.DMA,
+        ],
+        compiler_params=LIMIT,
+        name="slices_and_queries",
+    )(far(keys), far(values), far(prompt_id), far(queries))
+    return results[:-1], results[-1]
 
 
 def contract(left, right, dims):
@@ -191,23 +214,26 @@
 
 
 def attend(query, pieces, prompt, state):
-    for piece in pieces:
-        score = contract(query, piece[0, prompt], ((1,), (1,)))
-        peak = jnp.max(score, axis=1, keepdims=True)
-        weight = jnp.exp2((score - peak) * WEIGHT_SCALE)
-        total = jnp.sum(weight, axis=1, keepdims=True)
-        part = contract(weight.astype(jnp.bfloat16), piece[1, prompt], ((1,), (0,)))
-        peak = jnp.broadcast_to(peak * SCALING, part.shape)
-        total = jnp.broadcast_to(total, part.shape)
-        if state is None:
-            state = (peak, total, part)
-        else:
-            best, mass, acc = state
-            top = jnp.maximum(best, peak)
-            old = jnp.exp(best - top)
-            new = jnp.exp(peak - top)
-            state = (top, mass * old + total * new, acc * old + part * new)
-    return state
+    scores = [contract(query, piece[0, prompt], ((1,), (1,))) for piece in pieces]
+    peaks = [jnp.max(score, axis=1, keepdims=True) for score in scores]
+    weights = [jnp.exp2((score - peak) * WEIGHT_SCALE) for score, peak in zip(scores, peaks)]
+    parts = [
+        contract(weight.astype(jnp.bfloat16), piece[1, prompt], ((1,), (0,)))
+        for weight, piece in zip(weights, pieces)
+    ]
+    totals = [jnp.sum(weight, axis=1, keepdims=True) for weight in weights]
+    shape = parts[0].shape
+    tops = [jnp.broadcast_to(peak * SCALING, shape) for peak in peaks]
+    masses = [jnp.broadcast_to(total, shape) for total in totals]
+    if state is not None:
+        tops.append(state[0])
+        masses.append(state[1])
+        parts.append(state[2])
+    top = functools.reduce(jnp.maximum, tops)
+    factors = [jnp.exp(t - top) for t in tops]
+    mass = functools.reduce(jnp.add, [m * f for m, f in zip(masses, factors)])
+    out = functools.reduce(jnp.add, [p * f for p, f in zip(parts, factors)])
+    return top, mass, out
 
 
 def find_places(ids, prompts, rows):
@@ -242,24 +268,7 @@
         total_ref[target, :] = total
         return carry
 
-    lax.fori_loop(0, prompts * chunks, step, 0)
-
-
-def next_kernel(chunk, sorted_ref, acc_in, peak_in, total_in, *refs):
-    pieces, (acc_ref, peak_ref, total_ref) = refs[:-3], refs[-3:]
-    prompts = pieces[0].shape[1]
-    chunks = sorted_ref.shape[0] // prompts // chunk
-
-    def step(index, carry):
-        target = pl.ds(pl.multiple_of(index * chunk, chunk), chunk)
-        state = (peak_in[target, :], total_in[target, :], acc_in[target, :])
-        peak, total, out = attend(sorted_ref[target, :], pieces, index // chunks, state)
-        acc_ref[target, :] = out
-        peak_ref[target, :] = peak
-        total_ref[target, :] = total
-        return carry
-
-    lax.fori_loop(0, prompts * chunks, step, 0)
+    lax.fori_loop(0, prompts * chunks, step, 0, unroll=2)
 
 
 def last_kernel(rows, chunk, place_ref, sorted_ref, acc_ref, peak_ref, total_ref, *refs):
@@ -282,7 +291,7 @@
         aux_scratch[target, :] = left_right(peak + jnp.log(total), code)
         return carry
 
-    lax.fori_loop(0, prompts * chunks, step, 0)
+    lax.fori_loop(0, prompts * chunks, step, 0, unroll=2)
 
     mask = diagonal(owned * rows)
     first_rows = lax.broadcasted_iota(jnp.int32, (AUX_ROWS, LANES), 0) < AUX_ROWS // 2
@@ -307,7 +316,7 @@
     prompts = pieces[0].shape[1]
     total = places.shape[0] * rows
     results = pl.pallas_call(
-        functools.partial(first_kernel, rows, min(256, total // prompts)),
+        functools.partial(first_kernel, rows, min(512, total // prompts)),
         out_shape=[
             jax.ShapeDtypeStruct((total, HEAD_SIZE), jnp.bfloat16),
             jax.ShapeDtypeStruct((total, HEAD_SIZE), jnp.float32),
@@ -322,25 +331,11 @@
     return [near(result) for result in results]
 
 
-def next_stage(state, pieces):
-    total = state[0].shape[0]
-    prompts = pieces[0].shape[1]
-    results = pl.pallas_call(
-        functools.partial(next_kernel, min(256, total // prompts)),
-        out_shape=[jax.ShapeDtypeStruct((total, HEAD_SIZE), jnp.float32)] * 3,
-        in_specs=[whole()] * (4 + len(pieces)),
-        out_specs=[whole()] * 3,
-        compiler_params=LIMIT,
-        name="next_stage",
-    )(*state, *pieces)
-    return [state[0]] + [near(result) for result in results]
-
-
 def last_stage(places, state, pieces, rows, devices):
     prompts = pieces[0].shape[1]
     total = places.shape[0] * rows
     return pl.pallas_call(
-        functools.partial(last_kernel, rows, min(256, total // prompts)),
+        functools.partial(last_kernel, rows, min(512, total // prompts)),
         out_shape=jax.ShapeDtypeStruct((devices, total // devices + AUX_ROWS, HEAD_SIZE), jnp.int16),
         in_specs=[whole(pltpu.SMEM)] + [whole()] * (4 + len(pieces)),
         out_specs=whole(),
@@ -421,18 +416,21 @@
         route = [(i, i ^ partner) for i in range(devices)]
         arrived[partner] = near(lax.ppermute(piece, "seq", route))
 
-    slices = head_slices(document_keys, document_values, EARLY + LATE + (0,))
+    slices = head_slices(document_keys, document_values, FIRST)
+    exchange(slices[0], FIRST[0])
+    slices, packed = slices_and_queries(
+        document_keys, document_values, EARLY + LATE + (0,), queries, prompt_id, devices
+    )
     for partner, piece in zip(EARLY, slices):
         exchange(piece, partner)
-    packed = pack_queries(queries, prompt_id, devices)
     head_queries = lax.all_to_all(packed, "seq", split_axis=0, concat_axis=0, tiled=True)
     arrived[0] = near(slices[-1])
     for partner, piece in zip(LATE, slices[len(EARLY) :]):
         exchange(piece, partner)
     head_ids = head_queries[:, owned * rows, :owned].reshape(-1).astype(jnp.int32)
     places = find_places(head_ids, document_keys.shape[0], rows)
-    state = first_stage(places, near(head_queries), [arrived[k] for k in (0, 6, 7)], rows)
-    state = next_stage(state, [arrived[k] for k in (1, 4, 2)])
+    ready = [arrived[k] for k in (0, 6, 7, 1, 4, 2)]
+    state = first_stage(places, near(head_queries), ready, rows)
     sent = last_stage(places, state, [arrived[k] for k in (5, 3)], rows, devices)
     local, local_aux = suffix_part(
         suffix_len, packed, far(sample_keys), far(sample_values), step_keys, step_values

time: 62.9 us -> 60.9 us (0.968)
  Pallas kernels: 26.4 us -> 21.5 us
  waiting for transfers between devices: 15.6 us -> 19.1 us
    pallas_call x4 -> x3, Pallas kernels: 13.1 us -> 9.76 us  [the longest x1 3.66 us: first_stage(): pl.pallas_call(functools.partial(first_kernel, rows, min(512, total // pr...]
    ppermute x7, waiting for transfers between devices: 11.6 us -> 14.6 us  [exchange(): arrived[partner] = near(lax.ppermute(piece, 'seq', route))]
    pallas_call x1, Pallas kernels: 2.51 us -> 1 us  [head_slices(): pl.pallas_call(functools.partial(slice_kernel, partners), out_shape=[piec...]
    all_to_all x1, waiting for transfers between devices: 2.59 us -> 3.62 us  [body(): lax.all_to_all(packed, 'seq', split_axis=0, concat_axis=0, tiled=True)]
  transfers between devices with their start and end apart: 9 -> 9, of which waited for: 8 -> 8; matrix products, arithmetic and copies ran while one was open for 0% -> 0% of each run, Pallas kernels for 30% -> 24%
where the time goes in v2:
time: 60.9 us; the launch traced here: 60.4 us
  Pallas kernels  21.5 us (35%)
  starting transfers between devices  19.4 us (32%)
  waiting for transfers between devices  19.1 us (31%)
    ppermute x7, waiting for transfers between devices, exchange(): arrived[partner] = near(lax.ppermute(piece, 'seq', route))  14.6 us
    pallas_call x1, Pallas kernels, suffix_part(): pl.pallas_call(suffix_kernel, grid_spec=pltpu.PrefetchScalarGridSpec(num_...  9.6 us
    all_to_all x1, starting transfers between devices, body(): lax.all_to_all(packed, 'seq', split_axis=0, concat_axis=0, tiled=True)  7.56 us
    ppermute x7, starting transfers between devices, exchange(): arrived[partner] = near(lax.ppermute(piece, 'seq', route))  7.33 us
    all_to_all x1, starting transfers between devices, body(): lax.all_to_all(sent, 'seq', split_axis=0, concat_axis=0, tiled=True)  4.47 us
    pallas_call x1, Pallas kernels, first_stage(): pl.pallas_call(functools.partial(first_kernel, rows, min(512, total // pr...  3.66 us
    all_to_all x1, waiting for transfers between devices, body(): lax.all_to_all(packed, 'seq', split_axis=0, concat_axis=0, tiled=True)  3.62 us
    pallas_call x1, Pallas kernels, slices_and_queries(): pl.pallas_call(functools.partial(slice_and_pack_kernel, partners), out_sh...  3.25 us
  transfers between devices with their start and end apart: 9, of which 8 were waited for; matrix products, arithmetic and copies ran while one was open for 0% of the time, Pallas kernels for 24%

profile of v2, /device:TPU:0, one launch (start us, length us, event | category | flops | bytes accessed | tf_op | source)
XLA Modules:
  0.0 60.4 jit_solution(10729026768537960598)
XLA Ops:
  0.0 3.2 %slices_and_queries.1 = (bf16[2,2,256,128]{3,2,1,0:T(8,128)(2,1)}, bf16[2,2,256,128]{3,2,1,0:T(8,128)(2,1)S(1)}, bf16[2,2,256,128]{3,2,1,0:T(8,128)(2,1)S(1)}, b...) custom-call(bf16[2,256,1024]{2,1,0:T(8,128)(2,1)} %keys_ref.4, ...), custom_call_target="tpu_custom_call" | custom-call | tf_op jit(solution)/shard_map/slices_and_queries/pallas_call | solution.py:113
  3.3 0.0 copy-start
  3.3 0.0 copy-start.1
  3.3 0.0 copy-start.2
  3.3 7.6 %all-to-all-start = ((bf16[16,72,128]{2,1,0:T(8,128)(2,1)}), bf16[16,72,128]{2,1,0:T(8,128)(2,1)S(1)}, u32[]{:S(2)}, u32[]{:S(2)}) async-start(bf16[16,72,128]{2,1,0:T(8,128)(2,1)} %get-tuple-element.19.query_ref), calls=%async_computation | async-start | bytes 589824 | tf_op jit(solution)/shard_map/all_to_all | solution.py:426
  10.9 1.0 %head_slices.1 = bf16[2,2,256,128]{3,2,1,0:T(8,128)(2,1)S(1)} custom-call(bf16[2,256,1024]{2,1,0:T(8,128)(2,1)} %keys_ref.4, bf16[2,256,1024]{2,1,0:T(8,128)(2,1)} %values_ref.4), custom_call_target="tpu_custom_call" | custom-call | tf_op jit(solution)/shard_map/head_slices/pallas_call | solution.py:65
  11.9 2.9 %collective-permute-start = (bf16[2,2,256,128]{3,2,1,0:T(8,128)(2,1)S(1)}, bf16[2,2,256,128]{3,2,1,0:T(8,128)(2,1)S(1)}, u32[]{:S(2)}, u32[]{:S(2)}) collective-permute-start(bf16[2,2,256,128]{3,2,1,0:T(8,128)(2,1)S(1)} %head_slices.1), channel_id=1, source_target_pairs={{0,6},{1,7},{2,4},{3,5},{4,2},{5,3},{6,0},{7,1},{8,14},{9,15},{10,... | collective-permute-start | bytes 786440 | tf_op jit(solution)/shard_map/ppermute | solution.py:417
  14.7 0.0 collective-permute-start.1
  14.7 0.2 collective-permute-start.2
  15.0 1.9 %collective-permute-start.3 = (bf16[2,2,256,128]{3,2,1,0:T(8,128)(2,1)S(1)}, bf16[2,2,256,128]{3,2,1,0:T(8,128)(2,1)S(1)}, u32[]{:S(2)}, u32[]{:S(2)}) collective-permute-start(bf16[2,2,256,128]{3,2,1,0:T(8,128)(2,1)S(1)} %get-tuple-element.23), channel_id=1, source_target_pairs={{0,4},{1,5},{2,6},{3,7},{4,0},{5,1},{6,2},{7,3},{8,12},{9,13},{10,... | collective-permute-start | bytes 786440 | tf_op jit(solution)/shard_map/ppermute | solution.py:417
  16.9 1.5 %collective-permute-start.4 = (bf16[2,2,256,128]{3,2,1,0:T(8,128)(2,1)S(1)}, bf16[2,2,256,128]{3,2,1,0:T(8,128)(2,1)S(1)}, u32[]{:S(2)}, u32[]{:S(2)}) collective-permute-start(bf16[2,2,256,128]{3,2,1,0:T(8,128)(2,1)S(1)} %get-tuple-element.24), channel_id=1, source_target_pairs={{0,2},{1,3},{2,0},{3,1},{4,6},{5,7},{6,4},{7,5},{8,10},{9,11},{10,... | collective-permute-start | bytes 786440 | tf_op jit(solution)/shard_map/ppermute | solution.py:417
  18.4 3.6 %all-to-all-done.queries_ref = bf16[16,72,128]{2,1,0:T(8,128)(2,1)S(1)} async-done(((bf16[16,72,128]{2,1,0:T(8,128)(2,1)}), bf16[16,72,128]{2,1,0:T(8,128)(2,1)S(1)}, u32[]{:S(2)}, u32[]{:S(2)}) %all-to-all-start) | async-done | bytes 294944 | tf_op jit(solution)/shard_map/all_to_all | solution.py:426
  22.0 0.1 reshape.12
  22.1 3.7 %collective-permute-done.refs_1_ = bf16[2,2,256,128]{3,2,1,0:T(8,128)(2,1)S(1)} collective-permute-done((bf16[2,2,256,128]{3,2,1,0:T(8,128)(2,1)S(1)}, bf16[2,2,256,128]{3,2,1,0:T(8,128)(2,1)S(1)}, u32[]{:S(2)}, u32[]{:S(2)}) %collective-permute-start) | collective-permute-done | bytes 262176 | tf_op jit(solution)/shard_map/ppermute | solution.py:417
  25.8 0.0 collective-permute-start.5
  25.8 4.5 %collective-permute-done.1.refs_2_ = bf16[2,2,256,128]{3,2,1,0:T(8,128)(2,1)S(1)} collective-permute-done((bf16[2,2,256,128]{3,2,1,0:T(8,128)(2,1)}, bf16[2,2,256,128]{3,2,1,0:T(8,128)(2,1)S(1)}, u32[]{:S(2)}, u32[]{:S(2)}) %collective-permute-start.1) | collective-permute-done | bytes 262176 | tf_op jit(solution)/shard_map/ppermute | solution.py:417
  30.3 0.8 %collective-permute-start.6 = (bf16[2,2,256,128]{3,2,1,0:T(8,128)(2,1)S(1)}, bf16[2,2,256,128]{3,2,1,0:T(8,128)(2,1)S(1)}, u32[]{:S(2)}, u32[]{:S(2)}) collective-permute-start(bf16[2,2,256,128]{3,2,1,0:T(8,128)(2,1)S(1)} %get-tuple-element.30), channel_id=1, source_target_pairs={{0,3},{1,2},{2,1},{3,0},{4,7},{5,6},{6,5},{7,4},{8,11},{9,10},{10,... | collective-permute-start | bytes 786440 | tf_op jit(solution)/shard_map/ppermute | solution.py:417
  31.1 0.2 convert_reduce_fusion
  31.3 0.0 collective-permute-done.2.refs_3_
  31.3 4.5 %collective-permute-done.3.refs_4_ = bf16[2,2,256,128]{3,2,1,0:T(8,128)(2,1)S(1)} collective-permute-done((bf16[2,2,256,128]{3,2,1,0:T(8,128)(2,1)S(1)}, bf16[2,2,256,128]{3,2,1,0:T(8,128)(2,1)S(1)}, u32[]{:S(2)}, u32[]{:S(2)}) %collective-permute-start.3) | collective-permute-done | bytes 262176 | tf_op jit(solution)/shard_map/ppermute | solution.py:417
  35.8 0.4 collective-permute-done.4.refs_5_
  36.2 3.7 %first_stage.1 = (bf16[1024,128]{1,0:T(8,128)(2,1)S(1)}, f32[1024,128]{1,0:T(8,128)S(1)}, f32[1024,128]{1,0:T(8,128)S(1)}, f32[1024,128]{1,0:T(8,128)S(1)}) custom-call(s32[32]{0:T(128)S(1)} %add_multiply_fusion.place_ref, bf16[16,72,128]{2,1,0:T(8,128)(2,1)S(1)} %all-to-all-done.queries_ref, bf16[2,2,256,128]{3,2,1,0:T(8,128)(2,1)S(1)} %get-tuple-element.20.refs_0_, ...), custom_call_target="tpu_custom_call" | custom-call | tf_op jit(solution)/shard_map/first_stage/pallas_call | solution.py:318
  39.9 1.0 %collective-permute-done.5.refs_0_ = bf16[2,2,256,128]{3,2,1,0:T(8,128)(2,1)S(1)} collective-permute-done((bf16[2,2,256,128]{3,2,1,0:T(8,128)(2,1)S(1)}, bf16[2,2,256,128]{3,2,1,0:T(8,128)(2,1)S(1)}, u32[]{:S(2)}, u32[]{:S(2)}) %collective-permute-start.5) | collective-permute-done | bytes 262176 | tf_op jit(solution)/shard_map/ppermute | solution.py:417
  40.9 0.5 collective-permute-done.6.refs_1_
  41.4 2.9 %last_stage.1 = s16[16,72,128]{2,1,0:T(8,128)(2,1)} custom-call(s32[32]{0:T(128)S(1)} %add_multiply_fusion.place_ref, bf16[1024,128]{1,0:T(8,128)(2,1)S(1)} %get-tuple-element.25.sorted_ref, f32[1024,128]{1,0:T(8,128)S(1)} %get-tuple-element.26.acc_ref, f32[1024,128]{1,0:T(8,128)S(1)} %get-tuple-element.27.peak_ref, ...), custom_call_target="tpu_custom_call" | custom-call | tf_op jit(solution)/shard_map/last_stage/pallas_call | solution.py:337
  44.2 4.5 %all-to-all-start.1 = ((s16[16,72,128]{2,1,0:T(8,128)(2,1)}), s16[16,72,128]{2,1,0:T(8,128)(2,1)S(1)}, u32[]{:S(2)}, u32[]{:S(2)}) async-start(s16[16,72,128]{2,1,0:T(8,128)(2,1)} %last_stage.1), calls=%async_computation.1 | async-start | bytes 589824 | tf_op jit(solution)/shard_map/all_to_all | solution.py:438
  48.7 0.0 copy-done
  48.7 0.0 copy-done.1
  48.7 0.0 copy-done.2
  48.7 9.6 %suffix_part.1 = (f32[8,64,128]{2,1,0:T(8,128)S(1)}, f32[8,1,128]{2,1,0:T(1,128)S(1)}) custom-call(s32[2]{0:T(128)S(1)} %copy-done.2, bf16[16,72,128]{2,1,0:T(8,128)(2,1)} %get-tuple-element.19.query_ref, bf16[2,1024,1024]{2,1,0:T(8,128)(2,1)} %keys_ref.5, bf16[2,1024,1024]{2,1,0:T(8,128)(2,1)} %values_ref.5, bf16[2,4,1024]{2,1,0:T(4,128)(2,1)S(1)} %copy-done, ...), custom_call_target="tpu_custom_call" | custom-call | tf_op jit(solution)/shard_map/suffix_part/pallas_call | solution.py:190
  58.3 0.9 %all-to-all-done.1.got_ref = s16[16,72,128]{2,1,0:T(8,128)(2,1)S(1)} async-done(((s16[16,72,128]{2,1,0:T(8,128)(2,1)}), s16[16,72,128]{2,1,0:T(8,128)(2,1)S(1)}, u32[]{:S(2)}, u32[]{:S(2)}) %all-to-all-start.1) | async-done | bytes 294944 | tf_op jit(solution)/shard_map/all_to_all | solution.py:438
  59.2 1.1 %merge.1 = bf16[2,4,8192]{2,1,0:T(4,128)(2,1)} custom-call(s16[16,72,128]{2,1,0:T(8,128)(2,1)S(1)} %all-to-all-done.1.got_ref, f32[8,64,128]{2,1,0:T(8,128)S(1)} %get-tuple-element.31.local_ref, f32[8,1,128]{2,1,0:T(1,128)S(1)} %get-tuple-element.32.local_aux_ref), custom_call_target="tpu_custom_call" | custom-call | tf_op jit(solution)/shard_map/merge/pallas_call | solution.py:388
  (2 shorter events, 0.0 us)
Async XLA Ops:
  3.3 45.4 %copy-start = (bf16[2,4,1024]{2,1,0:T(4,128)(2,1)S(1)}, bf16[2,4,1024]{2,1,0:T(4,128)(2,1)}, u32[]{:S(2)}) copy-start(bf16[2,4,1024]{2,1,0:T(4,128)(2,1)} %new_keys_ref.1) | copy-start | bytes 49156
  3.3 45.4 %copy-start.1 = (bf16[2,4,1024]{2,1,0:T(4,128)(2,1)S(1)}, bf16[2,4,1024]{2,1,0:T(4,128)(2,1)}, u32[]{:S(2)}) copy-start(bf16[2,4,1024]{2,1,0:T(4,128)(2,1)} %new_values_ref.1) | copy-start | bytes 49156
  3.3 45.4 %copy-start.2 = (s32[2]{0:T(128)S(1)}, s32[2]{0:T(128)}, u32[]{:S(2)}) copy-start(s32[2]{0:T(128)} %len_ref.1) | copy-start | bytes 28
  3.3 18.7 %all-to-all-start = ((bf16[16,72,128]{2,1,0:T(8,128)(2,1)}), bf16[16,72,128]{2,1,0:T(8,128)(2,1)S(1)}, u32[]{:S(2)}, u32[]{:S(2)}) async-start(bf16[16,72,128]{2,1,0:T(8,128)(2,1)} %get-tuple-element.19.query_ref), calls=%async_computation | async-start | bytes 589824 | tf_op jit(solution)/shard_map/all_to_all | solution.py:426
  11.9 13.9 %collective-permute-start = (bf16[2,2,256,128]{3,2,1,0:T(8,128)(2,1)S(1)}, bf16[2,2,256,128]{3,2,1,0:T(8,128)(2,1)S(1)}, u32[]{:S(2)}, u32[]{:S(2)}) collective-permute-start(bf16[2,2,256,128]{3,2,1,0:T(8,128)(2,1)S(1)} %head_slices.1), channel_id=1, source_target_pairs={{0,6},{1,7},{2,4},{3,5},{4,2},{5,3},{6,0},{7,1},{8,14},{9,15},{10,... | collective-permute-start | bytes 786440 | tf_op jit(solution)/shard_map/ppermute | solution.py:417
  14.7 15.5 %collective-permute-start.1 = (bf16[2,2,256,128]{3,2,1,0:T(8,128)(2,1)}, bf16[2,2,256,128]{3,2,1,0:T(8,128)(2,1)S(1)}, u32[]{:S(2)}, u32[]{:S(2)}) collective-permute-start(bf16[2,2,256,128]{3,2,1,0:T(8,128)(2,1)} %get-tuple-element.21), channel_id=1, source_target_pairs={{0,7},{1,6},{2,5},{3,4},{4,3},{5,2},{6,1},{7,0},{8,15},{9,14},{10,... | collective-permute-start | bytes 786440 | tf_op jit(solution)/shard_map/ppermute | solution.py:417
  14.7 16.5 %collective-permute-start.2 = (bf16[2,2,256,128]{3,2,1,0:T(8,128)(2,1)S(1)}, bf16[2,2,256,128]{3,2,1,0:T(8,128)(2,1)S(1)}, u32[]{:S(2)}, u32[]{:S(2)}) collective-permute-start(bf16[2,2,256,128]{3,2,1,0:T(8,128)(2,1)S(1)} %get-tuple-element.22), channel_id=1, source_target_pairs={{0,1},{1,0},{2,3},{3,2},{4,5},{5,4},{6,7},{7,6},{8,9},{9,8},{10,11... | collective-permute-start | bytes 786440 | tf_op jit(solution)/shard_map/ppermute | solution.py:417
  15.0 20.9 %collective-permute-start.3 = (bf16[2,2,256,128]{3,2,1,0:T(8,128)(2,1)S(1)}, bf16[2,2,256,128]{3,2,1,0:T(8,128)(2,1)S(1)}, u32[]{:S(2)}, u32[]{:S(2)}) collective-permute-start(bf16[2,2,256,128]{3,2,1,0:T(8,128)(2,1)S(1)} %get-tuple-element.23), channel_id=1, source_target_pairs={{0,4},{1,5},{2,6},{3,7},{4,0},{5,1},{6,2},{7,3},{8,12},{9,13},{10,... | collective-permute-start | bytes 786440 | tf_op jit(solution)/shard_map/ppermute | solution.py:417
  16.9 19.4 %collective-permute-start.4 = (bf16[2,2,256,128]{3,2,1,0:T(8,128)(2,1)S(1)}, bf16[2,2,256,128]{3,2,1,0:T(8,128)(2,1)S(1)}, u32[]{:S(2)}, u32[]{:S(2)}) collective-permute-start(bf16[2,2,256,128]{3,2,1,0:T(8,128)(2,1)S(1)} %get-tuple-element.24), channel_id=1, source_target_pairs={{0,2},{1,3},{2,0},{3,1},{4,6},{5,7},{6,4},{7,5},{8,10},{9,11},{10,... | collective-permute-start | bytes 786440 | tf_op jit(solution)/shard_map/ppermute | solution.py:417
  25.8 15.1 %collective-permute-start.5 = (bf16[2,2,256,128]{3,2,1,0:T(8,128)(2,1)S(1)}, bf16[2,2,256,128]{3,2,1,0:T(8,128)(2,1)S(1)}, u32[]{:S(2)}, u32[]{:S(2)}) collective-permute-start(bf16[2,2,256,128]{3,2,1,0:T(8,128)(2,1)S(1)} %get-tuple-element.29), channel_id=1, source_target_pairs={{0,5},{1,4},{2,7},{3,6},{4,1},{5,0},{6,3},{7,2},{8,13},{9,12},{10,... | collective-permute-start | bytes 786440 | tf_op jit(solution)/shard_map/ppermute | solution.py:417
  30.3 11.1 %collective-permute-start.6 = (bf16[2,2,256,128]{3,2,1,0:T(8,128)(2,1)S(1)}, bf16[2,2,256,128]{3,2,1,0:T(8,128)(2,1)S(1)}, u32[]{:S(2)}, u32[]{:S(2)}) collective-permute-start(bf16[2,2,256,128]{3,2,1,0:T(8,128)(2,1)S(1)} %get-tuple-element.30), channel_id=1, source_target_pairs={{0,3},{1,2},{2,1},{3,0},{4,7},{5,6},{6,5},{7,4},{8,11},{9,10},{10,... | collective-permute-start | bytes 786440 | tf_op jit(solution)/shard_map/ppermute | solution.py:417
  44.2 15.0 %all-to-all-start.1 = ((s16[16,72,128]{2,1,0:T(8,128)(2,1)}), s16[16,72,128]{2,1,0:T(8,128)(2,1)S(1)}, u32[]{:S(2)}, u32[]{:S(2)}) async-start(s16[16,72,128]{2,1,0:T(8,128)(2,1)} %last_stage.1), calls=%async_computation.1 | async-start | bytes 589824 | tf_op jit(solution)/shard_map/all_to_all | solution.py:438
